TPU v7x, 256 devices: a whole 4x4x8 slice. The times are simulated.
256 devices in a mesh: dp: 4 (over x), expert: 64 (over y, z, core).
Axes of the slice: x: 4, y: 4, z: 8, core: 2. Of those that a mesh axis runs over, the one named last changes fastest.
Arguments:
- frames: bfloat16 [32768, 1024], P(('dp', 'expert')), may hold values from -6 to 6
- lengths: int32 [256], P(('dp', 'expert')), may hold values from 64 to 128
- expert_ids: int32 [32768, 2], P(('dp', 'expert')), may hold values from 0 to 63, all different within a row
- conv_in: bfloat16 [1024, 2048], P(('dp', 'expert')), may hold values from -0.1875 to 0.1875
- depthwise: bfloat16 [1024, 31], P(('dp', 'expert')), may hold values from -1 to 1
- router: bfloat16 [1024, 64], P(('dp', 'expert')), may hold values from -0.1875 to 0.1875
- w_in: bfloat16 [64, 1024, 4096], P('expert', None, 'dp'), may hold values from -0.1875 to 0.1875
- w_out: bfloat16 [64, 4096, 1024], P('expert', 'dp'), may hold values from -0.09375 to 0.09375
- out_grad: bfloat16 [32768, 1024], P(('dp', 'expert')), may hold values from -6 to 6
Outputs:
- layer_out: bfloat16 [32768, 1024], P(('dp', 'expert'))
- frames_grad: bfloat16 [32768, 1024], P(('dp', 'expert'))
- conv_in_grad: float32 [1024, 2048], P(('dp', 'expert'))
- depthwise_grad: float32 [1024, 31], P(('dp', 'expert'))
- router_grad: float32 [1024, 64], P(('dp', 'expert'))
- w_in_grad: bfloat16 [64, 1024, 4096], P('expert', None, 'dp')
- w_out_grad: bfloat16 [64, 4096, 1024], P('expert', 'dp')
Inputs may be any that keep to these rules, and one draw needn't show every extreme that they name: `expert_ids`: each frame names 2 different experts, and every expert is named by some frame.
All inputs are finite; a program needn't handle non-finite values.
Results may differ from a plain program's by a relative error of at most 0.019.
Values may be sent and summed in bfloat16 or wider, within the bound.
A program may use at most 128 MiB of HBM per device.

v0:
```python
import jax
import jax.numpy as jnp
from jax import lax
from jax.experimental import pallas as pl
from jax.experimental.pallas import tpu as pltpu
from jax.sharding import PartitionSpec as P

TOP = 2
KERNEL = 31


EPSILON = 1e-05


def swish_of(values):
    return values * jax.nn.sigmoid(values)


def swish_slope(values):
    sigmoid_v = jax.nn.sigmoid(values)
    return sigmoid_v * (1.0 + values * (1.0 - sigmoid_v))


def normalize(values):
    center = values - jnp.mean(values, axis=-1, keepdims=True)
    inv_scale = lax.rsqrt(jnp.mean(center * center, axis=-1, keepdims=True) + EPSILON)
    return (center * inv_scale, inv_scale)


def norm_backward(upstream, centred, inv_scale):
    first_mean = jnp.mean(upstream, axis=-1, keepdims=True)
    second_mean = jnp.mean(upstream * centred, axis=-1, keepdims=True)
    return inv_scale * (upstream - first_mean - centred * second_mean)


def pad_time(signal, half_width):
    return jnp.pad(signal, ((half_width, half_width), (0, 0)))


def depth_apply(signal, tap_rows, half_width):
    length = signal.shape[0]
    padded = pad_time(signal, half_width)
    summed = jnp.zeros(signal.shape, jnp.float32)
    for tap_index in range(tap_rows.shape[0]):
        summed = summed + tap_rows[tap_index] * lax.slice_in_dim(
            padded, tap_index, tap_index + length, axis=0
        )
    return summed


def depth_transpose(upstream, tap_rows, half_width):
    length = upstream.shape[0]
    padded = pad_time(upstream, half_width)
    summed = jnp.zeros(upstream.shape, jnp.float32)
    for tap_index in range(tap_rows.shape[0]):
        begin = 2 * half_width - tap_index
        summed = summed + tap_rows[tap_index] * lax.slice_in_dim(
            padded, begin, begin + length, axis=0
        )
    return summed


def depth_taps_grad(upstream, signal, half_width):
    length = signal.shape[0]
    padded = pad_time(signal, half_width)
    rows_list = []
    for tap_index in range(2 * half_width + 1):
        piece = lax.slice_in_dim(padded, tap_index, tap_index + length, axis=0)
        rows_list.append(jnp.sum(upstream * piece, axis=0))
    return jnp.stack(rows_list, axis=0)


def routing(choices, length, experts, capacity):
    tokens, top_count = choices.shape
    usable = jnp.arange(tokens, dtype=jnp.int32) < length
    flat_ids = choices.reshape(-1)
    live = jnp.repeat(usable, top_count)
    onehot = (flat_ids[:, None] == jnp.arange(experts, dtype=jnp.int32)[None, :]) & live[:, None]
    onehot_int = onehot.astype(jnp.int32)
    before = jnp.cumsum(onehot_int, axis=0) - onehot_int
    position = jnp.sum(jnp.where(onehot, before, 0), axis=1)
    kept_rows = live & (position < capacity)
    slot_total = experts * capacity
    slot_index = jnp.where(kept_rows, flat_ids * capacity + position, slot_total)
    match = slot_index[None, :] == jnp.arange(slot_total, dtype=jnp.int32)[:, None]
    filled = jnp.any(match, axis=1)
    source = jnp.sum(
        jnp.where(match, jnp.arange(tokens * top_count, dtype=jnp.int32)[None, :], 0), axis=1
    )
    return (usable, kept_rows, jnp.minimum(slot_index, slot_total - 1), filled, source)


MESH = pl.DeviceIdType.MESH
HALF = 1152
WIDE = 2 * HALF
SPLIT = 640
VMEM_LIMIT = 60 * 1024 * 1024


def place():
    x = lax.axis_index("dp")
    e = lax.axis_index("expert")
    return x, e // 16, (e // 2) % 8, e % 2


def spot(x, y, z, c):
    return (x, y * 16 + z * 2 + c)


def remote(src, dst, send, recv, where):
    return pltpu.make_async_remote_copy(
        src_ref=src, dst_ref=dst, send_sem=send, recv_sem=recv, device_id=where, device_id_type=MESH
    )


def greet(targets):
    barrier = pltpu.get_barrier_semaphore()
    for where in targets:
        pl.semaphore_signal(barrier, inc=1, device_id=where, device_id_type=MESH)
    pl.semaphore_wait(barrier, len(targets))


def axis_peers(x, y, z, c):
    peers = [spot(x, y, z, 1 - c)]
    peers += [spot(x, y, (z + dz) % 8, c) for dz in range(1, 8)]
    peers += [spot(x, (y + dy) % 4, z, c) for dy in (1, 3)]
    peers += [spot((x + dx) % 4, y, z, c) for dx in (1, 3)]
    return peers


def gather_kernel(own_ref, out_ref, core_s, core_r, own_sem, z_s, z_r, ring_s, ring_r, tail_s, tail_r):
    x, y, z, c = place()
    greet(axis_peers(x, y, z, c))
    partner = spot(x, y, z, 1 - c)
    mine = pl.multiple_of(c * HALF, 128)
    other = pl.multiple_of((1 - c) * HALF, 128)
    row = pl.multiple_of(y * 64 + z * 8, 8)
    row4 = pl.multiple_of(row + 4 * c, 4)
    swap = remote(
        own_ref.at[:, pl.ds(other, HALF)],
        out_ref.at[x, pl.ds(row4, 4), pl.ds(other, HALF)],
        core_s,
        core_r,
        partner,
    )
    swap.start()
    keep = pltpu.make_async_copy(
        own_ref.at[:, pl.ds(mine, HALF)], out_ref.at[x, pl.ds(row4, 4), pl.ds(mine, HALF)], own_sem
    )
    keep.start()
    keep.wait()
    swap.wait()
    copies = []
    for dz in (4, 3, 5, 2, 6, 1, 7):
        block = out_ref.at[x, pl.ds(row, 8), pl.ds(mine, HALF)]
        copy = remote(block, block, z_s.at[dz - 1], z_r.at[dz - 1], spot(x, y, (z + dz) % 8, c))
        copy.start()
        copies.append(copy)
    for copy in copies:
        copy.wait()

    first = pl.multiple_of(mine, 128)
    second = pl.multiple_of(mine + SPLIT, 128)
    yrow = pl.multiple_of(y * 64, 64)

    def block_of(colour, level, index, part):
        cols = pl.ds(first, SPLIT) if colour == 0 else pl.ds(second, HALF - SPLIT)
        if level == 0:
            height = 64 if part is None else 32
            offset = 0 if part is None else part * 32
            if colour == 0:
                return out_ref.at[x, pl.ds(pl.multiple_of(index * 64 + offset, 32), height), cols]
            return out_ref.at[index, pl.ds(pl.multiple_of(yrow + offset, 32), height), cols]
        if colour == 0:
            height = 256 if part is None else 128
            offset = 0 if part is None else part * 128
            return out_ref.at[index, pl.ds(offset, height), cols]
        height = 64 if part is None else 32
        offset = 0 if part is None else part * 32
        return out_ref.at[:, pl.ds(pl.multiple_of(index * 64 + offset, 32), height), cols]

    def whereto(colour, level, step):
        if (colour + level) % 2 == 0:
            return spot(x, (y + step) % 4, z, c)
        return spot((x + step) % 4, y, z, c)

    def position(colour, level):
        return y if (colour + level) % 2 == 0 else x

    def opened(colour, level):
        at = position(colour, level)
        block = block_of(colour, level, at, None)
        base = (colour * 2 + level) * 4
        right = remote(block, block, ring_s.at[base], ring_r.at[base], whereto(colour, level, 1))
        left = remote(block, block, ring_s.at[base + 1], ring_r.at[base + 1], whereto(colour, level, 3))
        right.start()
        left.start()
        return right, left

    def passed(colour, level, pair, tell):
        at = position(colour, level)
        base = (colour * 2 + level) * 4
        right, left = pair
        right.wait_recv()
        block = block_of(colour, level, (at + 3) % 4, 0)
        on_right = remote(block, block, ring_s.at[base + 2], ring_r.at[base + 2], whereto(colour, level, 1))
        on_right.start()
        tell((at + 3) % 4, 1)
        left.wait_recv()
        block = block_of(colour, level, (at + 1) % 4, 1)
        on_left = remote(block, block, ring_s.at[base + 3], ring_r.at[base + 3], whereto(colour, level, 3))
        on_left.start()
        tell((at + 1) % 4, 2)
        return on_right, on_left

    def closed(colour, level, pair, onward, tell):
        at = position(colour, level)
        for copy in onward:
            copy.wait_recv()
        tell((at + 2) % 4, 3)
        for copy in pair + onward:
            copy.wait_send()

    silent = lambda index, slot: None
    low = [opened(colour, 0) for colour in (0, 1)]
    low_on = [passed(colour, 0, low[colour], silent) for colour in (0, 1)]
    for colour in (0, 1):
        closed(colour, 0, low[colour], low_on[colour], silent)
    tails = []

    def teller(colour):
        def tell(index, slot):
            block = block_of(colour, 1, index, None)
            at = colour * 4 + slot
            copy = remote(block, block, tail_s.at[at], tail_r.at[at], partner)
            copy.start()
            tails.append(copy)

        return tell

    high = [opened(colour, 1) for colour in (0, 1)]
    for colour in (0, 1):
        teller(colour)(position(colour, 1), 0)
    high_on = [passed(colour, 1, high[colour], teller(colour)) for colour in (0, 1)]
    for colour in (0, 1):
        closed(colour, 1, high[colour], high_on[colour], teller(colour))
    for copy in tails:
        copy.wait()


def gather_weights(packed):
    dma = pltpu.SemaphoreType.DMA
    return pl.pallas_call(
        gather_kernel,
        out_shape=jax.ShapeDtypeStruct((4, 256, WIDE), jnp.bfloat16),
        in_specs=[pl.BlockSpec(memory_space=pltpu.VMEM)],
        out_specs=pl.BlockSpec(memory_space=pltpu.VMEM),
        scratch_shapes=[dma, dma, dma, dma((7,)), dma((7,)), dma((16,)), dma((16,)), dma((8,)), dma((8,))],
        compiler_params=pltpu.CompilerParams(
            collective_id=0, has_side_effects=True, vmem_limit_bytes=VMEM_LIMIT
        ),
        name="gather_weights",
    )(packed)


def reduce_kernel(
    part_ref, out_ref, swap_buf, half_buf, far_buf, near_buf, mid_buf, mid_far, mid_near, z_src, z_buf, last_src,
    last_buf, swap_s, swap_r, ring_s, ring_r, z_s, z_r, last_s, last_r
):
    x, y, z, c = place()
    greet(axis_peers(x, y, z, c))
    partner = spot(x, y, z, 1 - c)
    mine = pl.multiple_of(c * HALF, 128)
    other = pl.multiple_of((1 - c) * HALF, 128)
    colours = ((0, SPLIT), (SPLIT, HALF - SPLIT))
    order = (2, 1, 3, 0)

    def rows_of(colour, index):
        if colour == 0:
            return index, pl.ds(0, 256)
        return slice(None), pl.ds(pl.multiple_of(index * 64, 64), 64)

    swaps = {}
    for step in order:
        for colour, (begin, width) in enumerate(colours):
            at = ((x if colour == 0 else y) + step) % 4
            lead, rows = rows_of(colour, at)
            slot = colour * 4 + step
            copy = remote(
                part_ref.at[lead, rows, pl.ds(pl.multiple_of(other + begin, 128), width)],
                swap_buf.at[lead, rows, pl.ds(begin, width)],
                swap_s.at[slot],
                swap_r.at[slot],
                partner,
            )
            copy.start()
            swaps[colour, step] = copy

    def first_to(colour, step):
        if colour == 0:
            return spot((x + step) % 4, y, z, c)
        return spot(x, (y + step) % 4, z, c)

    def second_to(colour, step):
        return first_to(1 - colour, step)

    def fold(colour, step, extra):
        begin, width = colours[colour]
        at = ((x if colour == 0 else y) + step) % 4
        swaps[colour, step].wait_recv()

        def body(t, carry):
            if colour == 0:
                lead, row = at, pl.multiple_of(t * 32, 32)
            else:
                lead, row = t // 2, pl.multiple_of(at * 64 + (t % 2) * 32, 32)
            value = part_ref[lead, pl.ds(row, 32), pl.ds(pl.multiple_of(mine + begin, 128), width)].astype(jnp.float32)
            value = value + swap_buf[lead, pl.ds(row, 32), pl.ds(begin, width)].astype(jnp.float32)
            value = extra(t, value)
            half_buf[colour, step, pl.ds(pl.multiple_of(t * 32, 32), 32), pl.ds(0, width)] = value.astype(jnp.bfloat16)
            return carry

        return body

    plain = lambda t, value: value
    sent = []
    pend = {}
    for colour, (begin, width) in enumerate(colours):
        lax.fori_loop(0, 8, fold(colour, 2, plain), 0)
        for side, step in ((0, 1), (1, 3)):
            slot = colour * 8 + side
            copy = remote(
                half_buf.at[colour, 2, pl.ds(side * 128, 128), pl.ds(0, width)],
                far_buf.at[colour, side, :, pl.ds(0, width)],
                ring_s.at[slot],
                ring_r.at[slot],
                first_to(colour, step),
            )
            copy.start()
            pend[colour, side] = copy
            sent.append(copy)
    for colour, (begin, width) in enumerate(colours):
        for side, step in ((0, 1), (1, 3)):
            lo = side * 4

            lax.fori_loop(4 - lo, 8 - lo, fold(colour, step, plain), 0)
            pend[colour, side].wait_recv()

            def extra(t, value, colour=colour, side=side, lo=lo, width=width):
                row = pl.multiple_of((t - lo) * 32, 32)
                return value + far_buf[colour, side, pl.ds(row, 32), pl.ds(0, width)].astype(jnp.float32)

            def again(t, carry, colour=colour, step=step, extra=extra, begin=begin, width=width):
                at = ((x if colour == 0 else y) + step) % 4
                if colour == 0:
                    lead, row = at, pl.multiple_of(t * 32, 32)
                else:
                    lead, row = t // 2, pl.multiple_of(at * 64 + (t % 2) * 32, 32)
                value = part_ref[lead, pl.ds(row, 32), pl.ds(pl.multiple_of(mine + begin, 128), width)].astype(jnp.float32)
                value = value + swap_buf[lead, pl.ds(row, 32), pl.ds(begin, width)].astype(jnp.float32)
                value = extra(t, value)
                half_buf[colour, step, pl.ds(pl.multiple_of(t * 32, 32), 32), pl.ds(0, width)] = value.astype(jnp.bfloat16)
                return carry

            lax.fori_loop(lo, lo + 4, again, 0)
            slot = colour * 8 + 2 + side
            copy = remote(
                half_buf.at[colour, step, :, pl.ds(0, width)],
                near_buf.at[colour, side, :, pl.ds(0, width)],
                ring_s.at[slot],
                ring_r.at[slot],
                first_to(colour, step),
            )
            copy.start()
            pend[colour, 2 + side] = copy
            sent.append(copy)
    for colour, (begin, width) in enumerate(colours):
        pend[colour, 2].wait_recv()
        pend[colour, 3].wait_recv()

        def extra(t, value, colour=colour, width=width):
            row = pl.multiple_of(t * 32, 32)
            for side in (0, 1):
                value = value + near_buf[colour, side, pl.ds(row, 32), pl.ds(0, width)].astype(jnp.float32)
            return value

        body = fold(colour, 0, extra)
        lax.fori_loop(0, 8, body, 0)
        at = y if colour == 0 else x
        for side, step in ((0, 1), (1, 3)):
            row = pl.multiple_of(((at + 2) % 4) * 64 + side * 32, 32)
            slot = colour * 8 + 4 + side
            copy = remote(
                half_buf.at[colour, 0, pl.ds(row, 32), pl.ds(0, width)],
                mid_far.at[colour, side, :, pl.ds(0, width)],
                ring_s.at[slot],
                ring_r.at[slot],
                second_to(colour, step),
            )
            copy.start()
            pend[colour, 4 + side] = copy
            sent.append(copy)
    for colour, (begin, width) in enumerate(colours):
        at = y if colour == 0 else x
        for side, step in ((0, 1), (1, 3)):
            row = pl.multiple_of(((at + step) % 4) * 64, 32)
            pend[colour, 4 + side].wait_recv()
            for piece in (0, 1):
                value = half_buf[colour, 0, pl.ds(pl.multiple_of(row + piece * 32, 32), 32), pl.ds(0, width)]
                if piece == side:
                    value = value.astype(jnp.float32) + mid_far[colour, side, :, pl.ds(0, width)].astype(jnp.float32)
                    value = value.astype(jnp.bfloat16)
                mid_buf[colour, side, pl.ds(piece * 32, 32), pl.ds(0, width)] = value
            slot = colour * 8 + 6 + side
            copy = remote(
                mid_buf.at[colour, side, :, pl.ds(0, width)],
                mid_near.at[colour, side, :, pl.ds(0, width)],
                ring_s.at[slot],
                ring_r.at[slot],
                second_to(colour, step),
            )
            copy.start()
            pend[colour, 6 + side] = copy
            sent.append(copy)
    for colour, (begin, width) in enumerate(colours):
        at = y if colour == 0 else x
        pend[colour, 6].wait_recv()
        pend[colour, 7].wait_recv()
        for piece in range(2):
            rows = pl.ds(piece * 32, 32)
            value = half_buf[colour, 0, pl.ds(pl.multiple_of(at * 64 + piece * 32, 32), 32), pl.ds(0, width)].astype(jnp.float32)
            for side in (0, 1):
                value = value + mid_near[colour, side, rows, pl.ds(0, width)].astype(jnp.float32)
            z_src[pl.ds(piece * 4, 4), :, pl.ds(begin, width)] = value.astype(jnp.bfloat16).reshape(4, 8, width)
    z_copies = []
    for dz in (4, 3, 5, 2, 6, 1, 7):
        to = (z + dz) % 8
        copy = remote(z_src.at[to], z_buf.at[dz - 1], z_s.at[dz - 1], z_r.at[dz - 1], spot(x, y, to, c))
        copy.start()
        z_copies.append(copy)
    total = z_src[z].astype(jnp.float32)
    for copy in z_copies:
        copy.wait_recv()
    for k in range(7):
        total = total + z_buf[k].astype(jnp.float32)
    last_src[...] = total
    last = remote(last_src, last_buf, last_s, last_r, partner)
    last.start()
    for copy in sent + z_copies:
        copy.wait_send()
    for copy in swaps.values():
        copy.wait_send()
    out_ref[:, pl.ds(mine, HALF)] = jnp.where(c == 0, last_src[0:4, :], last_src[4:8, :])
    last.wait()
    out_ref[:, pl.ds(other, HALF)] = jnp.where(c == 0, last_buf[0:4, :], last_buf[4:8, :])


def reduce_grads(part):
    dma = pltpu.SemaphoreType.DMA
    bf, wide = jnp.bfloat16, SPLIT
    return pl.pallas_call(
        reduce_kernel,
        out_shape=jax.ShapeDtypeStruct((4, WIDE), jnp.float32),
        in_specs=[pl.BlockSpec(memory_space=pltpu.VMEM)],
        out_specs=pl.BlockSpec(memory_space=pltpu.VMEM),
        scratch_shapes=[
            pltpu.VMEM((4, 256, HALF), bf),
            pltpu.VMEM((2, 4, 256, wide), bf),
            pltpu.VMEM((2, 2, 128, wide), bf),
            pltpu.VMEM((2, 2, 256, wide), bf),
            pltpu.VMEM((2, 2, 64, wide), bf),
            pltpu.VMEM((2, 2, 32, wide), bf),
            pltpu.VMEM((2, 2, 64, wide), bf),
            pltpu.VMEM((8, 8, HALF), bf),
            pltpu.VMEM((7, 8, HALF), bf),
            pltpu.VMEM((8, HALF), jnp.float32),
            pltpu.VMEM((8, HALF), jnp.float32),
            dma((8,)),
            dma((8,)),
            dma((16,)),
            dma((16,)),
            dma((7,)),
            dma((7,)),
            dma,
            dma,
        ],
        compiler_params=pltpu.CompilerParams(
            collective_id=1, has_side_effects=True, vmem_limit_bytes=VMEM_LIMIT
        ),
        name="reduce_grads",
    )(part)


STEPS = (0, 1, 3, 2)


def expert_kernel(
    rows_ref, cot_ref, inner_hbm, outer_hbm, y_ref, z_ref, inner_grad_hbm, outer_grad_hbm,
    slots, cots, active, pre, inner, outer, part_y, part_z, straight_y, straight_z, relay_y, relay_z, joint_y, joint_z,
    grad_buf, sized, load_sem, self_s, there_s, there_r, ring_s, ring_r, fold_s, fold_r, back_s, back_r, store_sem
):
    x, y, z, c = place()
    f32, bf = jnp.float32, jnp.bfloat16
    here = y * 16 + z * 2 + c
    right, left, far = (x + 1) % 4, (x + 3) % 4, (x + 2) % 4
    to_right, to_left = spot(right, y, z, c), spot(left, y, z, c)
    loads = [
        pltpu.make_async_copy(inner_hbm, inner, load_sem.at[0]),
        pltpu.make_async_copy(outer_hbm, outer, load_sem.at[1]),
    ]
    for load in loads:
        load.start()

    barrier = pltpu.get_barrier_semaphore()

    def hail(i, carry):
        pl.semaphore_signal(barrier, inc=1, device_id=(x, (here + i) % 64), device_id_type=MESH)
        return carry

    lax.fori_loop(1, 64, hail, 0)
    for where in (to_right, to_left):
        pl.semaphore_signal(barrier, inc=1, device_id=where, device_id_type=MESH)
    pl.semaphore_wait(barrier, 65)

    own4 = pl.multiple_of(4 * here, 4)
    line4 = pl.multiple_of(8 * z + 4 * c, 4)
    kinds = ((rows_ref, slots), (cot_ref, cots))
    selfs = []
    for kind, (source, target) in enumerate(kinds):
        copy = pltpu.make_async_copy(
            source.at[pl.ds(own4, 4)], target.at[x, y, pl.ds(line4, 4)], self_s.at[kind]
        )
        copy.start()
        selfs.append(copy)
    for q, dy in enumerate(STEPS):
        yt = (y + 4 - dy) % 4

        def there(i, carry, yt=yt, q=q):
            zt, ct = (z + 4 + i // 2) % 8, (c + i) % 2
            et = yt * 16 + zt * 2 + ct
            rows = pl.ds(pl.multiple_of(4 * et, 4), 4)
            for kind, (source, target) in enumerate(kinds):
                remote(
                    source.at[rows], target.at[x, y, pl.ds(line4, 4)], there_s.at[kind, q], there_r.at[kind, q], (x, et)
                ).start()
            return carry

        if dy == 0:
            lax.fori_loop(0, 8, there, 0)
            lax.fori_loop(9, 16, there, 0)
        else:
            lax.fori_loop(0, 16, there, 0)

    def source_y(q):
        return (y + STEPS[q]) % 4

    rings = {}

    def arrive(q):
        ys = source_y(q)
        if STEPS[q] == 0:
            for copy in selfs:
                copy.wait()
        for kind, (_, target) in enumerate(kinds):
            view = sized.at[pl.ds(0, 15 if STEPS[q] == 0 else 16)]
            remote(view, view, there_s.at[kind, q], there_r.at[kind, q], to_right).wait_recv()
            block = target.at[x, ys]
            for side, where in ((0, to_right), (1, to_left)):
                copy = remote(block, block, ring_s.at[kind, side, q], ring_r.at[kind, side, q], where)
                copy.start()
                rings[kind, side, q] = copy

    def forward(q):
        ys = source_y(q)
        for kind, side, at, where in ((0, 0, left, to_right), (1, 1, right, to_left)):
            rings[kind, side, q].wait_recv()
            block = kinds[kind][1].at[at, ys]
            copy = remote(block, block, ring_s.at[kind, 2, q], ring_r.at[kind, 2, q], where)
            copy.start()
            rings[kind, 2, q] = copy

    folds = {}

    def push(name, q, source, target, where):
        copy = remote(source, target, fold_s.at[name, q], fold_r.at[name, q], where)
        copy.start()
        folds[name, q] = copy

    def compute(q):
        ys = source_y(q)
        rings[0, 1, q].wait_recv()
        rings[1, 0, q].wait_recv()
        rings[0, 2, q].wait_recv()
        rings[1, 2, q].wait_recv()

        def first(n, carry):
            cols = pl.ds(pl.multiple_of(n * 256, 256), 256)
            hidden = jnp.dot(slots[:, ys].reshape(256, 1024), inner[:, cols], preferred_element_type=f32)
            act_grad = lax.dot_general(
                cots[:, ys].reshape(256, 1024), outer[cols, :], (((1,), (1,)), ((), ())), preferred_element_type=f32
            )
            sig = jax.nn.sigmoid(hidden)
            active[:, ys, :, cols] = (hidden * sig).astype(bf).reshape(4, 64, 256)
            slope = sig * (1.0 + hidden * (1.0 - sig))
            pre[:, ys, :, cols] = (act_grad * slope).astype(bf).reshape(4, 64, 256)
            return carry

        lax.fori_loop(0, 4, first, 0)

        def second(n, carry):
            cols = pl.ds(pl.multiple_of(n * 256, 256), 256)
            out = jnp.dot(active[:, ys].reshape(256, 1024), outer[:, cols], preferred_element_type=f32)
            part_y[q, :, :, cols] = out.astype(bf).reshape(4, 64, 256)
            out = lax.dot_general(
                pre[:, ys].reshape(256, 1024), inner[cols, :], (((1,), (1,)), ((), ())), preferred_element_type=f32
            )
            part_z[q, :, :, cols] = out.astype(bf).reshape(4, 64, 256)
            return carry

        lax.fori_loop(0, 4, second, 0)
        push(2, q, part_y.at[q, far], relay_y.at[q], to_right)
        push(3, q, part_z.at[q, far], relay_z.at[q], to_left)
        push(0, q, part_z.at[q, right], straight_z.at[q], to_right)
        push(1, q, part_y.at[q, left], straight_y.at[q], to_left)

    def relay(q):
        folds[2, q].wait_recv()
        part_y[q, right] = (part_y[q, right].astype(f32) + relay_y[q].astype(f32)).astype(bf)
        push(4, q, part_y.at[q, right], joint_y.at[q], to_right)
        folds[3, q].wait_recv()
        part_z[q, left] = (part_z[q, left].astype(f32) + relay_z[q].astype(f32)).astype(bf)
        push(5, q, part_z.at[q, left], joint_z.at[q], to_left)

    def deliver(q):
        yt = source_y(q)
        for name in (1, 4, 0, 5):
            folds[name, q].wait_recv()
        part_y[q, x] = (part_y[q, x].astype(f32) + straight_y[q].astype(f32) + joint_y[q].astype(f32)).astype(bf)
        part_z[q, x] = (part_z[q, x].astype(f32) + straight_z[q].astype(f32) + joint_z[q].astype(f32)).astype(bf)

        def back(i, carry):
            zt, ct = (z + 4 + i // 2) % 8, (c + i) % 2
            rows = pl.ds(pl.multiple_of(8 * zt + 4 * ct, 4), 4)
            for kind, (source, target) in enumerate(((part_y, y_ref), (part_z, z_ref))):
                remote(
                    source.at[q, x, rows], target.at[pl.ds(own4, 4)], back_s.at[kind], back_r.at[kind], (x, yt * 16 + zt * 2 + ct)
                ).start()
            return carry

        if STEPS[q] == 0:
            lax.fori_loop(0, 8, back, 0)
            lax.fori_loop(9, 16, back, 0)
            for kind, (source, target) in enumerate(((part_y, y_ref), (part_z, z_ref))):
                copy = pltpu.make_async_copy(
                    source.at[q, x, pl.ds(line4, 4)], target.at[pl.ds(own4, 4)], self_s.at[2 + kind]
                )
                copy.start()
                selfs.append(copy)
        else:
            lax.fori_loop(0, 16, back, 0)

    stores = []

    def weight_grad(which, left_ref, right_ref, target):
        def body(n, carry):
            cols = pl.ds(pl.multiple_of(n * 256, 256), 256)
            out = lax.dot_general(
                left_ref[:, :, :, cols].reshape(1024, 256),
                right_ref[...].reshape(1024, 1024),
                (((0,), (0,)), ((), ())),
                preferred_element_type=f32,
            )
            grad_buf[which, cols, :] = out.astype(bf)
            return carry

        lax.fori_loop(0, 4, body, 0)
        copy = pltpu.make_async_copy(grad_buf.at[which], target, store_sem.at[which])
        copy.start()
        stores.append(copy)

    arrive(0)
    for load in loads:
        load.wait()
    arrive(1)
    forward(0)
    arrive(2)
    forward(1)
    compute(0)
    arrive(3)
    forward(2)
    compute(1)
    relay(0)
    forward(3)
    compute(2)
    relay(1)
    deliver(0)
    compute(3)
    relay(2)
    deliver(1)
    weight_grad(1, active, cots, outer_grad_hbm)
    relay(3)
    deliver(2)
    weight_grad(0, slots, pre, inner_grad_hbm)
    deliver(3)
    for kind in (0, 1):
        for q in range(4):
            view = sized.at[pl.ds(0, 15 if STEPS[q] == 0 else 16)]
            remote(view, view, there_s.at[kind, q], there_r.at[kind, q], to_right).wait_send()
    for copy in rings.values():
        copy.wait_send()
    for copy in folds.values():
        copy.wait_send()
    for kind in (0, 1):
        view = sized.at[pl.ds(0, 63)]
        remote(view, view, back_s.at[kind], back_r.at[kind], to_right).wait()
    for copy in selfs[2:] + stores:
        copy.wait()


def expert_pass(rows, cot, inner, outer):
    dma, bf = pltpu.SemaphoreType.DMA, jnp.bfloat16
    block = lambda *lead: pltpu.VMEM(lead + (64, 1024), bf)
    whole = jax.ShapeDtypeStruct((1024, 1024), bf)
    slot = jax.ShapeDtypeStruct((256, 1024), bf)
    vmem, anywhere = pl.BlockSpec(memory_space=pltpu.VMEM), pl.BlockSpec(memory_space=pl.ANY)
    return pl.pallas_call(
        expert_kernel,
        out_shape=(slot, slot, whole, whole),
        in_specs=[vmem, vmem, anywhere, anywhere],
        out_specs=(vmem, vmem, anywhere, anywhere),
        scratch_shapes=[block(4, 4)] * 4
        + [pltpu.VMEM((1024, 1024), bf)] * 2
        + [block(4, 4)] * 2
        + [block(4)] * 6
        + [pltpu.VMEM((2, 1024, 1024), bf), pltpu.VMEM((63, 4, 1024), bf)]
        + [
            dma((2,)),
            dma((4,)),
            dma((2, 4)),
            dma((2, 4)),
            dma((2, 3, 4)),
            dma((2, 3, 4)),
            dma((6, 4)),
            dma((6, 4)),
            dma((2,)),
            dma((2,)),
            dma((2,)),
        ],
        compiler_params=pltpu.CompilerParams(
            collective_id=2, has_side_effects=True, vmem_limit_bytes=VMEM_LIMIT
        ),
        name="expert_pass",
    )(rows, cot, inner, outer)


def per_device(frames, lengths, expert_ids, conv_in, depthwise, router, w_in, w_out, out_grad):
    tokens, width = frames.shape
    experts = router.shape[1]
    capacity = TOP * tokens // experts
    half_width = (KERNEL - 1) // 2
    packed = jnp.concatenate(
        [conv_in, router, jnp.pad(depthwise, ((0, 0), (0, WIDE - 2 * width - experts - KERNEL)))], axis=1
    )
    everything = gather_weights(packed).reshape(width, WIDE)
    conv_full = everything[:, : 2 * width]
    router_full = everything[:, 2 * width : 2 * width + experts]
    depth_full = everything[:, 2 * width + experts : 2 * width + experts + KERNEL]
    usable, kept_rows, slot_index, filled, source = routing(
        expert_ids, lengths[0], experts, capacity
    )
    frame_mask = usable.astype(jnp.float32)[:, None]
    frame_wide = frames.astype(jnp.float32)
    centred, inv_scale = normalize(frame_wide)
    normed = centred.astype(jnp.bfloat16)
    pointwise = jnp.dot(normed, conv_full, preferred_element_type=jnp.float32)
    value_half = pointwise[:, :width]
    gate_sig = jax.nn.sigmoid(pointwise[:, width:])
    gated = value_half * gate_sig * frame_mask
    tap_rows = depth_full.astype(jnp.float32).T
    conv_sum = depth_apply(gated, tap_rows, half_width)
    mixed_rows = (frame_wide + swish_of(conv_sum) * frame_mask).astype(jnp.bfloat16)
    logits = jnp.dot(mixed_rows, router_full, preferred_element_type=jnp.float32)
    onehots = (expert_ids[:, :, None] == jnp.arange(experts, dtype=jnp.int32)).astype(jnp.float32)
    chosen = jnp.sum(logits[:, None, :] * onehots, axis=-1)
    scores = jax.nn.sigmoid(chosen)
    score_sum = jnp.sum(scores, axis=-1, keepdims=True)
    weights = scores / score_sum
    kept_wide = kept_rows.reshape(tokens, TOP).astype(jnp.float32)
    send_rows = jnp.take(mixed_rows, source // TOP, axis=0)
    send_rows = jnp.where(filled[:, None], send_rows, jnp.zeros((), jnp.bfloat16)).reshape(
        experts, capacity, width
    )
    grad_wide = out_grad.astype(jnp.float32)
    slot_cot = (
        ((weights * kept_wide)[..., None] * grad_wide[:, None, :])
        .astype(jnp.bfloat16)
        .reshape(tokens * TOP, width)
    )
    cot_send = jnp.take(slot_cot, source, axis=0)
    cot_send = jnp.where(filled[:, None], cot_send, jnp.zeros((), jnp.bfloat16)).reshape(
        experts, capacity, width
    )
    expert_rows, back_rows, w_in_grad, w_out_grad = expert_pass(
        send_rows.reshape(-1, width), cot_send.reshape(-1, width), w_in[0], w_out[0]
    )
    picked = jnp.take(expert_rows, slot_index, axis=0).reshape(tokens, TOP, width)
    picked_wide = picked.astype(jnp.float32) * kept_wide[..., None]
    layer_out = (
        mixed_rows.astype(jnp.float32) + jnp.sum(weights[..., None] * picked_wide, axis=1)
    ).astype(jnp.bfloat16)
    conv_back, depth_back, router_back = conv_full, depth_full, router_full
    weight_grad = jnp.sum(grad_wide[:, None, :] * picked_wide, axis=-1)
    mean_term = jnp.sum(weight_grad * weights, axis=-1, keepdims=True)
    chosen_grad = (weight_grad - mean_term) / score_sum * scores * (1.0 - scores)
    logit_grad = jnp.sum(chosen_grad[..., None] * onehots, axis=1).astype(jnp.bfloat16)
    router_part = lax.dot_general(
        mixed_rows, logit_grad, (((0,), (0,)), ((), ())), preferred_element_type=jnp.float32
    )
    router_term = lax.dot_general(
        logit_grad, router_back, (((1,), (1,)), ((), ())), preferred_element_type=jnp.float32
    )
    slot_grad = jnp.take(back_rows, slot_index, axis=0).reshape(tokens, TOP, width)
    slot_grad = slot_grad.astype(jnp.float32) * kept_wide[..., None]
    mixed_grad = grad_wide + jnp.sum(slot_grad, axis=1) + router_term
    conv_grad = mixed_grad * frame_mask * swish_slope(conv_sum)
    tap_back = depth_back.astype(jnp.float32).T
    glu_grad = depth_transpose(conv_grad, tap_back, half_width) * frame_mask
    taps_grad = depth_taps_grad(conv_grad, gated, half_width)
    value_grad = glu_grad * gate_sig
    gate_grad = glu_grad * value_half * gate_sig * (1.0 - gate_sig)
    pre_cot = jnp.concatenate([value_grad, gate_grad], axis=-1).astype(jnp.bfloat16)
    conv_part = lax.dot_general(
        normed, pre_cot, (((0,), (0,)), ((), ())), preferred_element_type=jnp.float32
    )
    normed_grad = lax.dot_general(
        pre_cot, conv_back, (((1,), (1,)), ((), ())), preferred_element_type=jnp.float32
    )
    frames_grad = (mixed_grad + norm_backward(normed_grad, centred, inv_scale)).astype(jnp.bfloat16)
    small = jnp.concatenate(
        [router_part, taps_grad.T, jnp.zeros((width, WIDE - 2 * width - experts - KERNEL), jnp.float32)], axis=1
    )
    part = jnp.concatenate([conv_part.astype(jnp.bfloat16), small.astype(jnp.bfloat16)], axis=1)
    summed = reduce_grads(part.reshape(4, width // 4, WIDE))
    conv_in_grad = summed[:, : 2 * width]
    router_grad = summed[:, 2 * width : 2 * width + experts]
    depthwise_grad = summed[:, 2 * width + experts : 2 * width + experts + KERNEL]
    return (
        layer_out,
        frames_grad,
        conv_in_grad,
        depthwise_grad,
        router_grad,
        w_in_grad[None],
        w_out_grad[None],
    )


def solution(mesh):
    in_specs = (
        P(("dp", "expert"), None),
        P(("dp", "expert")),
        P(("dp", "expert"), None),
        P(("dp", "expert"), None),
        P(("dp", "expert"), None),
        P(("dp", "expert"), None),
        P("expert", None, "dp"),
        P("expert", "dp", None),
        P(("dp", "expert"), None),
    )
    out_specs = (
        P(("dp", "expert"), None),
        P(("dp", "expert"), None),
        P(("dp", "expert"), None),
        P(("dp", "expert"), None),
        P(("dp", "expert"), None),
        P("expert", None, "dp"),
        P("expert", "dp", None),
    )
    return jax.shard_map(
        per_device, mesh=mesh, in_specs=in_specs, out_specs=out_specs, check_vma=False
    )
```

profile of v0, /device:TPU:1, one launch (start us, length us, event | category | flops | bytes accessed | tf_op | source)
XLA Modules:
  0.0 259.4 jit_solution(14182231321179281340)
XLA Ops:
  1.3 1.1 convert_reduce_fusion
  2.4 1.2 fusion.14
  4.5 1.4 concatenate.13.own_ref
  8.8 1.2 mul.870
  10.8 42.8 %gather_weights.1 = bf16[4,256,2304]{2,1,0:T(8,128)(2,1)} custom-call(bf16[4,2304]{1,0:T(4,128)(2,1)} %concatenate.13.own_ref), custom_call_target="tpu_custom_call" | custom-call | tf_op jit(solution)/shard_map/gather_weights/pallas_call | solution.py:253
  53.6 1.1 slice.476
  55.0 3.0 %fusion.2 = f32[128,2048]{1,0:T(8,128)S(1)} fusion(bf16[1024,2304]{1,0:T(8,128)(2,1)} %bitcast.70, bf16[128,1024]{1,0:T(8,128)(2,1)S(1)} %copy-done.1, f32[128]{0:T(128)S(1)} %add_rsqrt_fusion, f32[128]{0:T(128)S(1)} %broadcast_multiply_fusion.2), kind=kOutput, calls=%fused_computation.7 | convolution fusion | flops 537395200 | bytes 5506048 | tf_op jit(solution)/shard_map/dot_general | solution.py:775
  58.9 2.9 %fusion.15 = (bf16[128,1024]{1,0:T(8,128)(2,1)S(1)}, f32[128,1024]{1,0:T(8,128)}) fusion(bf16[128,1024]{1,0:T(8,128)(2,1)S(1)} %copy-done.1, f32[128]{0:T(128)S(1)} %get-tuple-element.102, f32[1024]{0:T(1024)S(1)} %bitcast.105, f32[1024]{0:T(1024)S(1)} %bitcast.107, f32[1024]{0:T(1024)S(1)} %bitcast.109, f32[1024]{0:T(1024)S(1)} %bitcast.111, ...), kind=kLoop, calls=%fused_computation.89 | loop fusion | flops 9043968 | bytes 1700352 | tf_op jit(solution)/shard_map/convert_element_type | solution.py:781
  61.8 1.2 fusion.82
  63.4 2.0 gather_fusion
  65.5 2.0 gather_fusion.1
  67.4 2.4 select_select_fusion
  69.8 100.5 %expert_pass.1 = (bf16[256,1024]{1,0:T(8,128)(2,1)}, bf16[256,1024]{1,0:T(8,128)(2,1)}, bf16[1024,1024]{1,0:T(8,128)(2,1)}, bf16[1024,1024]{1,0:T(8,128)(2,1)}) custom-call(bf16[256,1024]{1,0:T(8,128)(2,1)} %get-tuple-element.98.rows_ref, bf16[256,1024]{1,0:T(8,128)(2,1)} %get-tuple-element.97.cot_ref, bf16[1024,1024]{1,0:T(8,128)(2,1)} %bitcast.74, ...), custom_call_target="tpu_custom_call" | custom-call | tf_op jit(solution)/shard_map/expert_pass/pallas_call | solution.py:726
  170.3 3.5 %gather_fusion.2 = bf16[256,1024]{1,0:T(8,128)(2,1)} fusion(bf16[256,1024]{1,0:T(8,128)(2,1)} %get-tuple-element.12, s32[1024]{0:T(1024)S(1)} %pad_clamp_fusion), kind=kCustom, calls=%fused_computation.1.clone | custom fusion | bytes 1049600 | tf_op jit(solution)/shard_map/jit(_take)/gather | solution.py:806
  173.8 1.4 multiply_reduce_fusion
  175.2 1.2 gather_fusion.3
  177.0 1.5 select_convert_fusion.1
  178.5 2.9 %reshape.304 = f32[128,2,1024]{2,1,0:T(2,128)} reshape(f32[256,1024]{1,0:T(8,128)} %get-tuple-element.95) | data formatting | bytes 2097152 | tf_op jit(solution)/shard_map/convert_element_type | solution.py:807
  181.5 2.8 %reshape.305 = f32[128,2,1024]{2,1,0:T(2,128)} reshape(f32[256,1024]{1,0:T(8,128)} %get-tuple-element.96) | data formatting | bytes 2097152 | tf_op jit(solution)/shard_map/convert_element_type | solution.py:823
  184.3 4.3 %multiply_reduce_fusion.1 = (f32[128,1024]{1,0:T(8,128)S(1)}, f32[128,1024]{1,0:T(8,128)S(1)}) fusion(f32[128,2,1024]{2,1,0:T(2,128)} %reshape.305, f32[128,2]{1,0:T(8,128)S(1)} %and_convert_fusion, f32[128,2,1024]{2,1,0:T(2,128)} %reshape.304, f32[128,2]{1,0:T(8,128)S(1)} %copy.76), kind=kLoop, calls=%fused_computation.72 | loop fusion | flops 1048576 | bytes 3147776 | tf_op jit(solution)/shard_map/reduce_sum | solution.py:824
  189.4 2.7 %multiply_reduce_fusion.3 = (bf16[1024]{0:T(1024)(128)(2,1)S(1)}, bf16[1024]{0:T(1024)(128)(2,1)S(1)}, bf16[1024]{0:T(1024)(128)(2,1)S(1)}, bf16[1024]{0:T(1024)...) fusion(f32[128,1024]{1,0:T(8,128)S(1)} %copy-done.4, ...), kind=kOutput, calls=%fused_computation.159 | convolution fusion | flops 23050240 | bytes 3199488 | tf_op jit(solution)/shard_map/dot_general | solution.py:819
  193.7 2.5 multiply_convert_fusion.2
  196.4 3.8 %fusion.98 = (f32[128]{0:T(128)S(1)}, f32[128]{0:T(128)S(1)}, f32[128,1024]{1,0:T(8,128)S(1)}) fusion(f32[128]{0:T(128)S(1)} %copy-done.8, f32[128]{0:T(128)S(1)} %broadcast_multiply_fusion.2, bf16[128,1024]{1,0:T(8,128)(2,1)S(1)} %copy-done.1, bf16[1024,2304]{1,0:T(8,128)(2,1)} %bitcast.73, bf16[128,1024]{1,0:T(8,128)(2,1)S(1)} %multiply_convert_fusion.1, ...), kind=kOutput, calls=%fused_computation.259 | convolution fusion | flops 538705664 | bytes 5507072 | tf_op jit(solution)/shard_map/dot_general | solution.py:835
  200.2 1.0 fusion.13
  201.2 3.4 %convolution_convert_fusion = bf16[1024,2048]{1,0:T(8,128)(2,1)} fusion(bf16[128,1024]{1,0:T(8,128)(2,1)S(1)} %multiply_convert_fusion.1, bf16[128,1024]{1,0:T(8,128)(2,1)S(1)} %get-tuple-element.52, bf16[128,1024]{1,0:T(8,128)(2,1)S(1)} %copy-done.1, f32[128]{0:T(128)S(1)} %copy-done.8, f32[128]{0:T(128)S(1)} %broadcast_multiply_fusion.2), kind=kOutput, calls=%fused_computation.4 | convolution fusion | flops 540540928 | bytes 4981760 | tf_op jit(solution)/shard_map/dot_general | solution.py:832
  204.6 7.9 %concatenate.15 = bf16[1024,2304]{1,0:T(8,128)(2,1)} concatenate(bf16[1024,2048]{1,0:T(8,128)(2,1)} %convolution_convert_fusion, bf16[1024,64]{1,0:T(8,128)(2,1)S(1)} %copy.84, bf16[1024,31]{1,0:T(8,128)(2,1)S(1)} %bitcast.78, bf16[1024,161]{1,0:T(8,128)(2,1)S(1)} %broadcast_in_dim.105), dimensions={1} | concatenate | bytes 9437184 | tf_op jit(solution)/shard_map/concatenate | solution.py:842
  212.5 38.6 %reduce_grads.1 = f32[4,2304]{1,0:T(4,128)} custom-call(bf16[4,256,2304]{2,1,0:T(8,128)(2,1)} %bitcast.68), custom_call_target="tpu_custom_call" | custom-call | tf_op jit(solution)/shard_map/reduce_grads/pallas_call | solution.py:461
  251.1 1.3 slice.467
  252.3 1.3 slice.466
  253.7 1.4 slice.465
  255.0 3.1 %copy.91 = bf16[1,1024,1024]{2,1,0:T(8,128)(2,1)} copy(bf16[1,1024,1024]{2,1,0:T(8,128)(2,1)} %bitcast.77) | data formatting | bytes 4194304
  258.1 1.3 copy.92
  (112 shorter events, 9.2 us)
Async XLA Ops:
  3.5 51.4 %copy-start.7 = (f32[128]{0:T(128)}, f32[128]{0:T(128)S(1)}, u32[]{:S(2)}) copy-start(f32[128]{0:T(128)S(1)} %add_rsqrt_fusion) | copy-start | bytes 1540
  3.6 54.6 %copy-start.9 = (f32[128]{0:T(128)}, f32[128]{0:T(128)S(1)}, u32[]{:S(2)}) copy-start(f32[128]{0:T(128)S(1)} %get-tuple-element.102) | copy-start | bytes 1540
  10.1 44.9 %copy-start.1 = (bf16[128,1024]{1,0:T(8,128)(2,1)S(1)}, bf16[128,1024]{1,0:T(8,128)(2,1)}, u32[]{:S(2)}) copy-start(bf16[128,1024]{1,0:T(8,128)(2,1)} %param.11) | copy-start | bytes 786436
  55.0 8.0 %copy-start.6 = (s32[128,2]{0,1:T(2,128)S(1)}, s32[128,2]{0,1:T(2,128)}, u32[]{:S(2)}) copy-start(s32[128,2]{0,1:T(2,128)} %param.13) | copy-start | bytes 3076
  58.1 0.8 copy-start.3
  170.3 4.9 %copy-start = (bf16[256,1024]{1,0:T(8,128)(2,1)S(1)}, bf16[256,1024]{1,0:T(8,128)(2,1)}, u32[]{:S(2)}) copy-start(bf16[256,1024]{1,0:T(8,128)(2,1)} %get-tuple-element.13) | copy-start | bytes 1572868
  175.2 1.8 copy-start.2
  178.5 10.8 %copy-start.4 = (f32[128,1024]{1,0:T(8,128)S(1)}, f32[128,1024]{1,0:T(8,128)}, u32[]{:S(2)}) copy-start(f32[128,1024]{1,0:T(8,128)} %copy-done.3) | copy-start | bytes 1572868
  189.4 4.4 %copy-start.10 = (f32[128]{0:T(128)S(1)}, f32[128]{0:T(128)}, u32[]{:S(2)}) copy-start(f32[128]{0:T(128)} %copy-done.9) | copy-start | bytes 1540
  192.1 4.3 %copy-start.8 = (f32[128]{0:T(128)S(1)}, f32[128]{0:T(128)}, u32[]{:S(2)}) copy-start(f32[128]{0:T(128)} %copy-done.7) | copy-start | bytes 1540
  212.5 45.6 %copy-start.5 = (bf16[1024,1024]{1,0:T(8,128)(2,1)S(1)}, bf16[1024,1024]{1,0:T(8,128)(2,1)}, u32[]{:S(2)}) copy-start(bf16[1024,1024]{1,0:T(8,128)(2,1)} %get-tuple-element.15) | copy-start | bytes 6291460
where the time goes:
time: 260 us; the launch traced here: 259 us
  Pallas kernels  182 us (70%)
  local copies, waits for them, and re-layouts  39.9 us (15%)
  other arithmetic  21.5 us (8%)
  matrix products  14.2 us (5%)
    pallas_call x1, Pallas kernels, expert_pass(): pl.pallas_call(expert_kernel, out_shape=(slot, slot, whole, whole), in_sp...  100 us
    pallas_call x1, Pallas kernels, gather_weights(): pl.pallas_call(gather_kernel, out_shape=jax.ShapeDtypeStruct((4, 256, WID...  42.8 us
    pallas_call x1, Pallas kernels, reduce_grads(): pl.pallas_call(reduce_kernel, out_shape=jax.ShapeDtypeStruct((4, WIDE), j...  38.6 us
    concatenate x1, local copies, waits for them, and re-layouts, per_device(): jnp.concatenate([conv_part.astype(jnp.bfloat16), small.astype(jnp.bfloat1...  7.9 us
    unnamed x26, local copies, waits for them, and re-layouts  6.19 us

commit v1 on v0

--- a/solution.py
+++ b/solution.py
@@ -5,10 +5,7 @@
 from jax.experimental.pallas import tpu as pltpu
 from jax.sharding import PartitionSpec as P
 
-TOP = 2
 KERNEL = 31
-
-
 EPSILON = 1e-05
 
 
@@ -25,69 +22,6 @@
     center = values - jnp.mean(values, axis=-1, keepdims=True)
     inv_scale = lax.rsqrt(jnp.mean(center * center, axis=-1, keepdims=True) + EPSILON)
     return (center * inv_scale, inv_scale)
-
-
-def norm_backward(upstream, centred, inv_scale):
-    first_mean = jnp.mean(upstream, axis=-1, keepdims=True)
-    second_mean = jnp.mean(upstream * centred, axis=-1, keepdims=True)
-    return inv_scale * (upstream - first_mean - centred * second_mean)
-
-
-def pad_time(signal, half_width):
-    return jnp.pad(signal, ((half_width, half_width), (0, 0)))
-
-
-def depth_apply(signal, tap_rows, half_width):
-    length = signal.shape[0]
-    padded = pad_time(signal, half_width)
-    summed = jnp.zeros(signal.shape, jnp.float32)
-    for tap_index in range(tap_rows.shape[0]):
-        summed = summed + tap_rows[tap_index] * lax.slice_in_dim(
-            padded, tap_index, tap_index + length, axis=0
-        )
-    return summed
-
-
-def depth_transpose(upstream, tap_rows, half_width):
-    length = upstream.shape[0]
-    padded = pad_time(upstream, half_width)
-    summed = jnp.zeros(upstream.shape, jnp.float32)
-    for tap_index in range(tap_rows.shape[0]):
-        begin = 2 * half_width - tap_index
-        summed = summed + tap_rows[tap_index] * lax.slice_in_dim(
-            padded, begin, begin + length, axis=0
-        )
-    return summed
-
-
-def depth_taps_grad(upstream, signal, half_width):
-    length = signal.shape[0]
-    padded = pad_time(signal, half_width)
-    rows_list = []
-    for tap_index in range(2 * half_width + 1):
-        piece = lax.slice_in_dim(padded, tap_index, tap_index + length, axis=0)
-        rows_list.append(jnp.sum(upstream * piece, axis=0))
-    return jnp.stack(rows_list, axis=0)
-
-
-def routing(choices, length, experts, capacity):
-    tokens, top_count = choices.shape
-    usable = jnp.arange(tokens, dtype=jnp.int32) < length
-    flat_ids = choices.reshape(-1)
-    live = jnp.repeat(usable, top_count)
-    onehot = (flat_ids[:, None] == jnp.arange(experts, dtype=jnp.int32)[None, :]) & live[:, None]
-    onehot_int = onehot.astype(jnp.int32)
-    before = jnp.cumsum(onehot_int, axis=0) - onehot_int
-    position = jnp.sum(jnp.where(onehot, before, 0), axis=1)
-    kept_rows = live & (position < capacity)
-    slot_total = experts * capacity
-    slot_index = jnp.where(kept_rows, flat_ids * capacity + position, slot_total)
-    match = slot_index[None, :] == jnp.arange(slot_total, dtype=jnp.int32)[:, None]
-    filled = jnp.any(match, axis=1)
-    source = jnp.sum(
-        jnp.where(match, jnp.arange(tokens * top_count, dtype=jnp.int32)[None, :], 0), axis=1
-    )
-    return (usable, kept_rows, jnp.minimum(slot_index, slot_total - 1), filled, source)
 
 
 MESH = pl.DeviceIdType.MESH
@@ -264,7 +198,7 @@
 
 
 def reduce_kernel(
-    part_ref, out_ref, swap_buf, half_buf, far_buf, near_buf, mid_buf, mid_far, mid_near, z_src, z_buf, last_src,
+    part_ref, out_ref, depth_ref, router_ref, swap_buf, half_buf, far_buf, near_buf, mid_buf, mid_far, mid_near, z_src, z_buf, last_src,
     last_buf, swap_s, swap_r, ring_s, ring_r, z_s, z_r, last_s, last_r
 ):
     x, y, z, c = place()
@@ -450,9 +384,14 @@
         copy.wait_send()
     for copy in swaps.values():
         copy.wait_send()
-    out_ref[:, pl.ds(mine, HALF)] = jnp.where(c == 0, last_src[0:4, :], last_src[4:8, :])
+    kept = jnp.where(c == 0, last_src[0:4, :], last_src[4:8, :])
     last.wait()
-    out_ref[:, pl.ds(other, HALF)] = jnp.where(c == 0, last_buf[0:4, :], last_buf[4:8, :])
+    got = jnp.where(c == 0, last_buf[0:4, :], last_buf[4:8, :])
+    low, high = jnp.where(c == 0, kept, got), jnp.where(c == 0, got, kept)
+    out_ref[:, 0:HALF] = low
+    out_ref[:, HALF:2048] = high[:, 0 : 2048 - HALF]
+    router_ref[...] = high[:, 2048 - HALF : 2112 - HALF]
+    depth_ref[...] = high[:, 2112 - HALF : 2112 + KERNEL - HALF]
 
 
 def reduce_grads(part):
@@ -460,9 +399,9 @@
     bf, wide = jnp.bfloat16, SPLIT
     return pl.pallas_call(
         reduce_kernel,
-        out_shape=jax.ShapeDtypeStruct((4, WIDE), jnp.float32),
+        out_shape=tuple(jax.ShapeDtypeStruct((4, width), jnp.float32) for width in (2048, KERNEL, 64)),
         in_specs=[pl.BlockSpec(memory_space=pltpu.VMEM)],
-        out_specs=pl.BlockSpec(memory_space=pltpu.VMEM),
+        out_specs=(pl.BlockSpec(memory_space=pltpu.VMEM),) * 3,
         scratch_shapes=[
             pltpu.VMEM((4, 256, HALF), bf),
             pltpu.VMEM((2, 4, 256, wide), bf),
@@ -753,97 +692,268 @@
     )(rows, cot, inner, outer)
 
 
+def columns_of(n, width):
+    return pl.ds(pl.multiple_of(n * width, width), width)
+
+
+def mask_of(length_ref):
+    return (lax.broadcasted_iota(jnp.int32, (128, 1), 0) < length_ref[0]).astype(jnp.float32)
+
+
+def chosen_of(ids_ref):
+    lane = lax.broadcasted_iota(jnp.int32, (128, 128), 1)
+    return [lane == ids_ref[:, k : k + 1] for k in (0, 1)]
+
+
+def identity():
+    shape = (128, 128)
+    return (lax.broadcasted_iota(jnp.int32, shape, 0) == lax.broadcasted_iota(jnp.int32, shape, 1)).astype(jnp.bfloat16)
+
+
+def front_kernel(
+    frames_ref, length_ref, ids_ref, og_ref, full_ref, rows_ref, cot_ref, mixed_ref, value_ref, sig_ref, conv_ref,
+    xhat_ref, notes_ref, gated_ref, taps_ref
+):
+    f32, bf = jnp.float32, jnp.bfloat16
+    mask = mask_of(length_ref)
+    xhat, inv_scale = normalize(frames_ref[...].astype(f32))
+    xhat_ref[...] = xhat
+    normed = xhat.astype(bf)
+    zeros = jnp.zeros((16, 1024), f32)
+    gated_ref[0:16, :] = zeros
+    gated_ref[144:160, :] = zeros
+
+    def point(n, carry):
+        cols = columns_of(n, 256)
+        value = jnp.dot(normed, full_ref[:, :, cols].reshape(1024, 256), preferred_element_type=f32)
+        gate = jnp.dot(normed, full_ref[:, :, columns_of(n + 4, 256)].reshape(1024, 256), preferred_element_type=f32)
+        sig = jax.nn.sigmoid(gate)
+        value_ref[:, cols] = value
+        sig_ref[:, cols] = sig
+        gated_ref[16:144, cols] = value * sig * mask
+        return carry
+
+    lax.fori_loop(0, 4, point, 0)
+    small = full_ref[:, :, 2048:2176].reshape(1024, 128)
+    taps_ref[...] = lax.dot_general(identity(), small, (((1,), (1,)), ((), ())), preferred_element_type=f32)
+
+    def depth(n, carry):
+        cols = columns_of(n, 128)
+        total = jnp.zeros((128, 128), f32)
+        for k in range(KERNEL):
+            total = total + taps_ref[64 + k : 65 + k, cols] * gated_ref[k + 1 : k + 129, cols]
+        conv_ref[:, cols] = total
+        mixed_ref[:, cols] = (frames_ref[:, cols].astype(f32) + swish_of(total) * mask).astype(bf)
+        return carry
+
+    lax.fori_loop(0, 8, depth, 0)
+    mixed = mixed_ref[...]
+    logits = jnp.dot(mixed, small, preferred_element_type=f32)
+    picks = chosen_of(ids_ref)
+    scores = [jax.nn.sigmoid(jnp.sum(jnp.where(pick, logits, 0.0), axis=1, keepdims=True)) for pick in picks]
+    score_sum = scores[0] + scores[1]
+    weights = [score / score_sum for score in scores]
+    count = (jnp.where(picks[0] | picks[1], 1.0, 0.0) * mask).astype(bf)
+    shape = (128, 128)
+    below = (lax.broadcasted_iota(jnp.int32, shape, 1) < lax.broadcasted_iota(jnp.int32, shape, 0)).astype(bf)
+    before = jnp.dot(below, count, preferred_element_type=f32)
+    wide = lax.broadcasted_iota(jnp.int32, (128, 256), 1).astype(f32)
+    slots, spots = [], []
+    for k, pick in enumerate(picks):
+        position = jnp.sum(jnp.where(pick, before, 0.0), axis=1, keepdims=True)
+        kept = (position < 4.0) & (mask > 0.0)
+        slot = jnp.where(kept, ids_ref[:, k : k + 1].astype(f32) * 4.0 + position, -1.0)
+        slots.append(slot)
+        spots.append((wide == slot).astype(bf))
+    lane = lax.broadcasted_iota(jnp.int32, shape, 1)
+    notes = jnp.zeros(shape, f32)
+    for i, column in enumerate(weights + scores + [score_sum] + slots + [inv_scale]):
+        notes = jnp.where(lane == i, column, notes)
+    notes_ref[...] = notes
+    both = spots[0] + spots[1]
+
+    def fill(n, carry):
+        cols = columns_of(n, 256)
+        down = (((0,), (0,)), ((), ()))
+        rows_ref[:, cols] = lax.dot_general(both, mixed_ref[:, cols], down, preferred_element_type=f32).astype(bf)
+        og = og_ref[:, cols].astype(f32)
+        total = jnp.zeros((256, 256), f32)
+        for k in (0, 1):
+            total = total + lax.dot_general(
+                spots[k], (weights[k] * og).astype(bf), down, preferred_element_type=f32
+            )
+        cot_ref[:, cols] = total.astype(bf)
+        return carry
+
+    lax.fori_loop(0, 4, fill, 0)
+
+
+def front(frames, lengths, ids, og, full):
+    bf, f32 = jnp.bfloat16, jnp.float32
+    vmem = pl.BlockSpec(memory_space=pltpu.VMEM)
+    shape = lambda *args: jax.ShapeDtypeStruct(*args)
+    return pl.pallas_call(
+        front_kernel,
+        out_shape=(
+            shape((256, 1024), bf), shape((256, 1024), bf), shape((128, 1024), bf), shape((128, 1024), f32),
+            shape((128, 1024), f32), shape((128, 1024), f32), shape((128, 1024), f32), shape((128, 128), f32),
+            shape((160, 1024), f32), shape((128, 1024), f32),
+        ),
+        in_specs=[vmem, pl.BlockSpec(memory_space=pltpu.SMEM), vmem, vmem, vmem],
+        out_specs=(vmem,) * 10,
+        compiler_params=pltpu.CompilerParams(vmem_limit_bytes=VMEM_LIMIT),
+        name="front",
+    )(frames, lengths, ids, og, full)
+
+
+def back_kernel(
+    y_ref, z_ref, og_ref, mixed_ref, value_ref, sig_ref, conv_ref, xhat_ref, notes_ref, gated_ref, taps_ref, length_ref,
+    ids_ref, full_ref, inner_ref, outer_ref, layer_ref, frames_ref, part_ref, inner_out, outer_out, pass_buf, pass_s,
+    mg_buf, cg_buf, tg_buf, pc_buf, turned, ng_buf
+):
+    f32, bf = jnp.float32, jnp.bfloat16
+    takes = [pltpu.make_async_copy(src, pass_buf.at[i], pass_s.at[i]) for i, src in enumerate((inner_ref, outer_ref))]
+    gives = [pltpu.make_async_copy(pass_buf.at[i], dst, pass_s.at[2 + i]) for i, dst in enumerate((inner_out, outer_out))]
+    for take in takes:
+        take.start()
+    mask = mask_of(length_ref)
+    picks = chosen_of(ids_ref)
+    notes = notes_ref[...]
+    column = lambda i: notes[:, i : i + 1]
+    weights, scores, score_sum, inv_scale = (column(0), column(1)), (column(2), column(3)), column(4), column(7)
+    wide = lax.broadcasted_iota(jnp.int32, (128, 256), 1).astype(f32)
+    spots = [(wide == column(5 + k)).astype(bf) for k in (0, 1)]
+    both = spots[0] + spots[1]
+
+    def output(n, carry):
+        cols = columns_of(n, 256)
+        og = og_ref[:, cols].astype(f32)
+        total = jnp.zeros((128, 256), f32)
+        sums = []
+        for k in (0, 1):
+            picked = jnp.dot(spots[k], y_ref[:, cols], preferred_element_type=f32)
+            total = total + weights[k] * picked
+            sums.append(carry[k] + jnp.sum(og * picked, axis=1, keepdims=True))
+        layer_ref[:, cols] = (mixed_ref[:, cols].astype(f32) + total).astype(bf)
+        return tuple(sums)
+
+    start = jnp.zeros((128, 1), f32)
+    weight_grad = lax.fori_loop(0, 4, output, (start, start))
+    mean_term = weight_grad[0] * weights[0] + weight_grad[1] * weights[1]
+    logit_grad = jnp.zeros((128, 128), f32)
+    for k in (0, 1):
+        chosen = (weight_grad[k] - mean_term) / score_sum * scores[k] * (1.0 - scores[k])
+        logit_grad = jnp.where(picks[k], chosen, logit_grad)
+    logit_grad = logit_grad.astype(bf)
+    zeros = jnp.zeros((16, 1024), f32)
+    cg_buf[0:16, :] = zeros
+    cg_buf[144:160, :] = zeros
+    across = (((1,), (1,)), ((), ()))
+
+    def mix(n, carry):
+        cols = columns_of(n, 256)
+        grad = og_ref[:, cols].astype(f32) + jnp.dot(both, z_ref[:, cols], preferred_element_type=f32)
+        grad = grad + lax.dot_general(logit_grad, full_ref[n, :, 2048:2176], across, preferred_element_type=f32)
+        mg_buf[:, cols] = grad
+        cg_buf[16:144, cols] = grad * mask * swish_slope(conv_ref[:, cols])
+        return carry
+
+    lax.fori_loop(0, 4, mix, 0)
+    tg_buf[...] = jnp.zeros((128, 1024), f32)
+
+    def depth(n, carry):
+        cols = columns_of(n, 128)
+        grad = cg_buf[16:144, cols]
+        total = jnp.zeros((128, 128), f32)
+        for k in range(KERNEL):
+            total = total + taps_ref[64 + k : 65 + k, cols] * cg_buf[31 - k : 159 - k, cols]
+            tg_buf[64 + k : 65 + k, cols] = jnp.sum(grad * gated_ref[k + 1 : k + 129, cols], axis=0, keepdims=True)
+        total = total * mask
+        sig = sig_ref[:, cols]
+        pc_buf[:, cols] = (total * sig).astype(bf)
+        pc_buf[:, columns_of(n + 8, 128)] = (total * value_ref[:, cols] * sig * (1.0 - sig)).astype(bf)
+        return carry
+
+    lax.fori_loop(0, 8, depth, 0)
+    for take in takes:
+        take.wait()
+    for give in gives:
+        give.start()
+    turned[...] = jnp.transpose(xhat_ref[...]).astype(bf)
+
+    def outer_product(n, carry):
+        cols = columns_of(n, 256)
+        out = jnp.dot(turned[...], pc_buf[:, cols], preferred_element_type=f32)
+        part_ref[:, :, cols] = out.astype(bf).reshape(4, 256, 256)
+        return carry
+
+    lax.fori_loop(0, 8, outer_product, 0)
+    down = (((0,), (0,)), ((), ()))
+    out = lax.dot_general(mixed_ref[...], logit_grad, down, preferred_element_type=f32)
+    out = out + lax.dot_general(tg_buf[...].astype(bf), identity(), down, preferred_element_type=f32)
+    part_ref[:, :, 2048:2176] = out.astype(bf).reshape(4, 256, 128)
+    part_ref[:, :, 2176:2304] = jnp.zeros((4, 256, 128), bf)
+
+    def inward(n, carry):
+        cols = columns_of(n, 256)
+        out = lax.dot_general(pc_buf[...], full_ref[n, :, 0:2048], across, preferred_element_type=f32)
+        ng_buf[:, cols] = out
+        first = carry[0] + jnp.sum(out, axis=1, keepdims=True)
+        second = carry[1] + jnp.sum(out * xhat_ref[:, cols], axis=1, keepdims=True)
+        return first, second
+
+    first, second = lax.fori_loop(0, 4, inward, (start, start))
+    first, second = first * (1.0 / 1024), second * (1.0 / 1024)
+
+    def finish(n, carry):
+        cols = columns_of(n, 256)
+        grad = inv_scale * (ng_buf[:, cols] - first - xhat_ref[:, cols] * second)
+        frames_ref[:, cols] = (mg_buf[:, cols] + grad).astype(bf)
+        return carry
+
+    lax.fori_loop(0, 4, finish, 0)
+    for give in gives:
+        give.wait()
+
+
+def backward(y, z, og, saved, lengths, ids, full, inner, outer):
+    bf, f32 = jnp.bfloat16, jnp.float32
+    vmem, anywhere = pl.BlockSpec(memory_space=pltpu.VMEM), pl.BlockSpec(memory_space=pl.ANY)
+    shape = lambda *args: jax.ShapeDtypeStruct(*args)
+    whole = shape((1024, 1024), bf)
+    return pl.pallas_call(
+        back_kernel,
+        out_shape=(shape((128, 1024), bf), shape((128, 1024), bf), shape((4, 256, WIDE), bf), whole, whole),
+        in_specs=[vmem] * 11 + [pl.BlockSpec(memory_space=pltpu.SMEM), vmem, vmem, anywhere, anywhere],
+        out_specs=(vmem, vmem, vmem, anywhere, anywhere),
+        scratch_shapes=[
+            pltpu.VMEM((2, 1024, 1024), bf),
+            pltpu.SemaphoreType.DMA((4,)),
+            pltpu.VMEM((128, 1024), f32),
+            pltpu.VMEM((160, 1024), f32),
+            pltpu.VMEM((128, 1024), f32),
+            pltpu.VMEM((128, 2048), bf),
+            pltpu.VMEM((1024, 128), bf),
+            pltpu.VMEM((128, 1024), f32),
+        ],
+        compiler_params=pltpu.CompilerParams(vmem_limit_bytes=VMEM_LIMIT),
+        name="backward",
+    )(y, z, og, *saved, lengths, ids, full, inner, outer)
+
+
 def per_device(frames, lengths, expert_ids, conv_in, depthwise, router, w_in, w_out, out_grad):
-    tokens, width = frames.shape
+    width = frames.shape[1]
     experts = router.shape[1]
-    capacity = TOP * tokens // experts
-    half_width = (KERNEL - 1) // 2
     packed = jnp.concatenate(
         [conv_in, router, jnp.pad(depthwise, ((0, 0), (0, WIDE - 2 * width - experts - KERNEL)))], axis=1
     )
-    everything = gather_weights(packed).reshape(width, WIDE)
-    conv_full = everything[:, : 2 * width]
-    router_full = everything[:, 2 * width : 2 * width + experts]
-    depth_full = everything[:, 2 * width + experts : 2 * width + experts + KERNEL]
-    usable, kept_rows, slot_index, filled, source = routing(
-        expert_ids, lengths[0], experts, capacity
+    full = gather_weights(packed)
+    rows, cot, *saved = front(frames, lengths, expert_ids, out_grad, full)
+    expert_rows, back_rows, inner, outer = expert_pass(rows, cot, w_in[0], w_out[0])
+    layer_out, frames_grad, part, w_in_grad, w_out_grad = backward(
+        expert_rows, back_rows, out_grad, saved, lengths, expert_ids, full, inner, outer
     )
-    frame_mask = usable.astype(jnp.float32)[:, None]
-    frame_wide = frames.astype(jnp.float32)
-    centred, inv_scale = normalize(frame_wide)
-    normed = centred.astype(jnp.bfloat16)
-    pointwise = jnp.dot(normed, conv_full, preferred_element_type=jnp.float32)
-    value_half = pointwise[:, :width]
-    gate_sig = jax.nn.sigmoid(pointwise[:, width:])
-    gated = value_half * gate_sig * frame_mask
-    tap_rows = depth_full.astype(jnp.float32).T
-    conv_sum = depth_apply(gated, tap_rows, half_width)
-    mixed_rows = (frame_wide + swish_of(conv_sum) * frame_mask).astype(jnp.bfloat16)
-    logits = jnp.dot(mixed_rows, router_full, preferred_element_type=jnp.float32)
-    onehots = (expert_ids[:, :, None] == jnp.arange(experts, dtype=jnp.int32)).astype(jnp.float32)
-    chosen = jnp.sum(logits[:, None, :] * onehots, axis=-1)
-    scores = jax.nn.sigmoid(chosen)
-    score_sum = jnp.sum(scores, axis=-1, keepdims=True)
-    weights = scores / score_sum
-    kept_wide = kept_rows.reshape(tokens, TOP).astype(jnp.float32)
-    send_rows = jnp.take(mixed_rows, source // TOP, axis=0)
-    send_rows = jnp.where(filled[:, None], send_rows, jnp.zeros((), jnp.bfloat16)).reshape(
-        experts, capacity, width
-    )
-    grad_wide = out_grad.astype(jnp.float32)
-    slot_cot = (
-        ((weights * kept_wide)[..., None] * grad_wide[:, None, :])
-        .astype(jnp.bfloat16)
-        .reshape(tokens * TOP, width)
-    )
-    cot_send = jnp.take(slot_cot, source, axis=0)
-    cot_send = jnp.where(filled[:, None], cot_send, jnp.zeros((), jnp.bfloat16)).reshape(
-        experts, capacity, width
-    )
-    expert_rows, back_rows, w_in_grad, w_out_grad = expert_pass(
-        send_rows.reshape(-1, width), cot_send.reshape(-1, width), w_in[0], w_out[0]
-    )
-    picked = jnp.take(expert_rows, slot_index, axis=0).reshape(tokens, TOP, width)
-    picked_wide = picked.astype(jnp.float32) * kept_wide[..., None]
-    layer_out = (
-        mixed_rows.astype(jnp.float32) + jnp.sum(weights[..., None] * picked_wide, axis=1)
-    ).astype(jnp.bfloat16)
-    conv_back, depth_back, router_back = conv_full, depth_full, router_full
-    weight_grad = jnp.sum(grad_wide[:, None, :] * picked_wide, axis=-1)
-    mean_term = jnp.sum(weight_grad * weights, axis=-1, keepdims=True)
-    chosen_grad = (weight_grad - mean_term) / score_sum * scores * (1.0 - scores)
-    logit_grad = jnp.sum(chosen_grad[..., None] * onehots, axis=1).astype(jnp.bfloat16)
-    router_part = lax.dot_general(
-        mixed_rows, logit_grad, (((0,), (0,)), ((), ())), preferred_element_type=jnp.float32
-    )
-    router_term = lax.dot_general(
-        logit_grad, router_back, (((1,), (1,)), ((), ())), preferred_element_type=jnp.float32
-    )
-    slot_grad = jnp.take(back_rows, slot_index, axis=0).reshape(tokens, TOP, width)
-    slot_grad = slot_grad.astype(jnp.float32) * kept_wide[..., None]
-    mixed_grad = grad_wide + jnp.sum(slot_grad, axis=1) + router_term
-    conv_grad = mixed_grad * frame_mask * swish_slope(conv_sum)
-    tap_back = depth_back.astype(jnp.float32).T
-    glu_grad = depth_transpose(conv_grad, tap_back, half_width) * frame_mask
-    taps_grad = depth_taps_grad(conv_grad, gated, half_width)
-    value_grad = glu_grad * gate_sig
-    gate_grad = glu_grad * value_half * gate_sig * (1.0 - gate_sig)
-    pre_cot = jnp.concatenate([value_grad, gate_grad], axis=-1).astype(jnp.bfloat16)
-    conv_part = lax.dot_general(
-        normed, pre_cot, (((0,), (0,)), ((), ())), preferred_element_type=jnp.float32
-    )
-    normed_grad = lax.dot_general(
-        pre_cot, conv_back, (((1,), (1,)), ((), ())), preferred_element_type=jnp.float32
-    )
-    frames_grad = (mixed_grad + norm_backward(normed_grad, centred, inv_scale)).astype(jnp.bfloat16)
-    small = jnp.concatenate(
-        [router_part, taps_grad.T, jnp.zeros((width, WIDE - 2 * width - experts - KERNEL), jnp.float32)], axis=1
-    )
-    part = jnp.concatenate([conv_part.astype(jnp.bfloat16), small.astype(jnp.bfloat16)], axis=1)
-    summed = reduce_grads(part.reshape(4, width // 4, WIDE))
-    conv_in_grad = summed[:, : 2 * width]
-    router_grad = summed[:, 2 * width : 2 * width + experts]
-    depthwise_grad = summed[:, 2 * width + experts : 2 * width + experts + KERNEL]
+    conv_in_grad, depthwise_grad, router_grad = reduce_grads(part)
     return (
         layer_out,
         frames_grad,

time: 260 us -> 221 us (0.85)
  local copies, waits for them, and re-layouts: 39.9 us -> 7.35 us
  Pallas kernels: 182 us -> 212 us
  other arithmetic: 21.5 us -> 0 us
  matrix products: 14.2 us -> 0 us
    pallas_call x1 -> x3, Pallas kernels: 38.6 us -> 68.7 us  [the longest x1 38.4 us: reduce_grads(): pl.pallas_call(reduce_kernel, out_shape=tuple((jax.ShapeDtypeStruct((4, w...]
    dot_general x6 -> x0, matrix products: 14.2 us -> none  [the longest x1 3.79 us: per_device(): lax.dot_general(pre_cot, conv_back, (((1,), (1,)), ((), ())), preferred_e...]
    reduce_sum x11 -> x0, other arithmetic: 9.03 us -> none  [the longest x1 4.33 us: per_device(): mixed_grad = grad_wide + jnp.sum(slot_grad, axis=1) + router_term]
    gather x4 -> x0, local copies, waits for them, and re-layouts: 8.61 us -> none  [the longest x1 3.52 us: per_device(): jnp.take(expert_rows, slot_index, axis=0).reshape(tokens, TOP, width)]
    concatenate x1 -> x0, local copies, waits for them, and re-layouts: 7.9 us -> none  [per_device(): jnp.concatenate([conv_part.astype(jnp.bfloat16), small.astype(jnp.bfloat1...]
    convert_element_type x8 -> x0, other arithmetic: 6.35 us -> none  [the longest x1 2.88 us: per_device(): (frame_wide + swish_of(conv_sum) * frame_mask).astype(jnp.bfloat16)]
    convert_element_type x2 -> x0, local copies, waits for them, and re-layouts: 5.73 us -> none  [the longest x1 2.92 us: per_device(): picked_wide = picked.astype(jnp.float32) * kept_wide[..., None]]
    slice x7 -> x0, local copies, waits for them, and re-layouts: 5.31 us -> none  [the longest x1 1.37 us: per_device(): conv_in_grad = summed[:, :2 * width]]
where the time goes in v1:
time: 221 us
  Pallas kernels  212 us (96%)
  local copies, waits for them, and re-layouts  7.35 us (3%)
    pallas_call x1, Pallas kernels, expert_pass(): pl.pallas_call(expert_kernel, out_shape=(slot, slot, whole, whole), in_sp...  100 us
    pallas_call x1, Pallas kernels, gather_weights(): pl.pallas_call(gather_kernel, out_shape=jax.ShapeDtypeStruct((4, 256, WID...  42.7 us
    pallas_call x1, Pallas kernels, reduce_grads(): pl.pallas_call(reduce_kernel, out_shape=tuple((jax.ShapeDtypeStruct((4, w...  38.4 us
    pallas_call x1, Pallas kernels, backward(): pl.pallas_call(back_kernel, out_shape=(shape((128, 1024), bf), shape((128...  19.6 us
    pallas_call x1, Pallas kernels, front(): pl.pallas_call(front_kernel, out_shape=(shape((256, 1024), bf), shape((25...  10.7 us
    unnamed x4, local copies, waits for them, and re-layouts  5.25 us

profile of v1, /device:TPU:1, one launch (start us, length us, event | category | flops | bytes accessed | tf_op | source)
XLA Modules:
  0.0 220.5 jit_solution(2889693803648096436)
XLA Ops:
  1.3 0.7 pad.4
  2.0 1.4 concatenate.3.own_ref
  3.4 1.4 copy.16.ids_ref
  4.8 42.7 %gather_weights.1.full_ref = bf16[4,256,2304]{2,1,0:T(8,128)(2,1)} custom-call(bf16[4,2304]{1,0:T(4,128)(2,1)} %concatenate.3.own_ref), custom_call_target="tpu_custom_call" | custom-call | tf_op jit(solution)/shard_map/gather_weights/pallas_call | solution.py:187
  47.5 10.7 %front.1 = (bf16[256,1024]{1,0:T(8,128)(2,1)}, bf16[256,1024]{1,0:T(8,128)(2,1)}, bf16[128,1024]{1,0:T(8,128)(2,1)}, f32[128,1024]{1,0:T(8,128)}, f32[128,1024]{...) custom-call(bf16[128,1024]{1,0:T(8,128)(2,1)} %frames_ref.1, ...), custom_call_target="tpu_custom_call" | custom-call | tf_op jit(solution)/shard_map/front/pallas_call | solution.py:795
  58.2 100.4 %expert_pass.1 = (bf16[256,1024]{1,0:T(8,128)(2,1)}, bf16[256,1024]{1,0:T(8,128)(2,1)}, bf16[1024,1024]{1,0:T(8,128)(2,1)}, bf16[1024,1024]{1,0:T(8,128)(2,1)}) custom-call(bf16[256,1024]{1,0:T(8,128)(2,1)} %get-tuple-element.29.rows_ref, bf16[256,1024]{1,0:T(8,128)(2,1)} %get-tuple-element.30.cot_ref, bf16[1024,1024]{1,0:T(8,128)(2,1)} %bitcast.4, ...), custom_call_target="tpu_custom_call" | custom-call | tf_op jit(solution)/shard_map/expert_pass/pallas_call | solution.py:665
  158.6 19.6 %backward.1 = (bf16[128,1024]{1,0:T(8,128)(2,1)}, bf16[128,1024]{1,0:T(8,128)(2,1)}, bf16[4,256,2304]{2,1,0:T(8,128)(2,1)}, bf16[1024,1024]{1,0:T(8,128)(2,1)}, bf16[1024,1024]{1,0:T(8,128)(2,1)}) custom-call(bf16[256,1024]{1,0:T(8,128)(2,1)} %get-tuple-element.31.y_ref, bf16[256,1024]{1,0:T(8,128)(2,1)} %get-tuple-element.32.z_ref, ...), custom_call_target="tpu_custom_call" | custom-call | tf_op jit(solution)/shard_map/backward/pallas_call | solution.py:924
  178.2 38.4 %reduce_grads.1 = (f32[4,2048]{1,0:T(4,128)}, f32[4,31]{1,0:T(4,128)}, f32[4,64]{1,0:T(4,128)}) custom-call(bf16[4,256,2304]{2,1,0:T(8,128)(2,1)} %get-tuple-element.45.part_ref), custom_call_target="tpu_custom_call" | custom-call | tf_op jit(solution)/shard_map/reduce_grads/pallas_call | solution.py:400
  216.7 1.4 copy.22
  218.0 1.2 copy.23
  219.3 1.2 copy.24

commit v2 on v1

--- a/solution.py
+++ b/solution.py
@@ -60,141 +60,6 @@
     peers += [spot(x, (y + dy) % 4, z, c) for dy in (1, 3)]
     peers += [spot((x + dx) % 4, y, z, c) for dx in (1, 3)]
     return peers
-
-
-def gather_kernel(own_ref, out_ref, core_s, core_r, own_sem, z_s, z_r, ring_s, ring_r, tail_s, tail_r):
-    x, y, z, c = place()
-    greet(axis_peers(x, y, z, c))
-    partner = spot(x, y, z, 1 - c)
-    mine = pl.multiple_of(c * HALF, 128)
-    other = pl.multiple_of((1 - c) * HALF, 128)
-    row = pl.multiple_of(y * 64 + z * 8, 8)
-    row4 = pl.multiple_of(row + 4 * c, 4)
-    swap = remote(
-        own_ref.at[:, pl.ds(other, HALF)],
-        out_ref.at[x, pl.ds(row4, 4), pl.ds(other, HALF)],
-        core_s,
-        core_r,
-        partner,
-    )
-    swap.start()
-    keep = pltpu.make_async_copy(
-        own_ref.at[:, pl.ds(mine, HALF)], out_ref.at[x, pl.ds(row4, 4), pl.ds(mine, HALF)], own_sem
-    )
-    keep.start()
-    keep.wait()
-    swap.wait()
-    copies = []
-    for dz in (4, 3, 5, 2, 6, 1, 7):
-        block = out_ref.at[x, pl.ds(row, 8), pl.ds(mine, HALF)]
-        copy = remote(block, block, z_s.at[dz - 1], z_r.at[dz - 1], spot(x, y, (z + dz) % 8, c))
-        copy.start()
-        copies.append(copy)
-    for copy in copies:
-        copy.wait()
-
-    first = pl.multiple_of(mine, 128)
-    second = pl.multiple_of(mine + SPLIT, 128)
-    yrow = pl.multiple_of(y * 64, 64)
-
-    def block_of(colour, level, index, part):
-        cols = pl.ds(first, SPLIT) if colour == 0 else pl.ds(second, HALF - SPLIT)
-        if level == 0:
-            height = 64 if part is None else 32
-            offset = 0 if part is None else part * 32
-            if colour == 0:
-                return out_ref.at[x, pl.ds(pl.multiple_of(index * 64 + offset, 32), height), cols]
-            return out_ref.at[index, pl.ds(pl.multiple_of(yrow + offset, 32), height), cols]
-        if colour == 0:
-            height = 256 if part is None else 128
-            offset = 0 if part is None else part * 128
-            return out_ref.at[index, pl.ds(offset, height), cols]
-        height = 64 if part is None else 32
-        offset = 0 if part is None else part * 32
-        return out_ref.at[:, pl.ds(pl.multiple_of(index * 64 + offset, 32), height), cols]
-
-    def whereto(colour, level, step):
-        if (colour + level) % 2 == 0:
-            return spot(x, (y + step) % 4, z, c)
-        return spot((x + step) % 4, y, z, c)
-
-    def position(colour, level):
-        return y if (colour + level) % 2 == 0 else x
-
-    def opened(colour, level):
-        at = position(colour, level)
-        block = block_of(colour, level, at, None)
-        base = (colour * 2 + level) * 4
-        right = remote(block, block, ring_s.at[base], ring_r.at[base], whereto(colour, level, 1))
-        left = remote(block, block, ring_s.at[base + 1], ring_r.at[base + 1], whereto(colour, level, 3))
-        right.start()
-        left.start()
-        return right, left
-
-    def passed(colour, level, pair, tell):
-        at = position(colour, level)
-        base = (colour * 2 + level) * 4
-        right, left = pair
-        right.wait_recv()
-        block = block_of(colour, level, (at + 3) % 4, 0)
-        on_right = remote(block, block, ring_s.at[base + 2], ring_r.at[base + 2], whereto(colour, level, 1))
-        on_right.start()
-        tell((at + 3) % 4, 1)
-        left.wait_recv()
-        block = block_of(colour, level, (at + 1) % 4, 1)
-        on_left = remote(block, block, ring_s.at[base + 3], ring_r.at[base + 3], whereto(colour, level, 3))
-        on_left.start()
-        tell((at + 1) % 4, 2)
-        return on_right, on_left
-
-    def closed(colour, level, pair, onward, tell):
-        at = position(colour, level)
-        for copy in onward:
-            copy.wait_recv()
-        tell((at + 2) % 4, 3)
-        for copy in pair + onward:
-            copy.wait_send()
-
-    silent = lambda index, slot: None
-    low = [opened(colour, 0) for colour in (0, 1)]
-    low_on = [passed(colour, 0, low[colour], silent) for colour in (0, 1)]
-    for colour in (0, 1):
-        closed(colour, 0, low[colour], low_on[colour], silent)
-    tails = []
-
-    def teller(colour):
-        def tell(index, slot):
-            block = block_of(colour, 1, index, None)
-            at = colour * 4 + slot
-            copy = remote(block, block, tail_s.at[at], tail_r.at[at], partner)
-            copy.start()
-            tails.append(copy)
-
-        return tell
-
-    high = [opened(colour, 1) for colour in (0, 1)]
-    for colour in (0, 1):
-        teller(colour)(position(colour, 1), 0)
-    high_on = [passed(colour, 1, high[colour], teller(colour)) for colour in (0, 1)]
-    for colour in (0, 1):
-        closed(colour, 1, high[colour], high_on[colour], teller(colour))
-    for copy in tails:
-        copy.wait()
-
-
-def gather_weights(packed):
-    dma = pltpu.SemaphoreType.DMA
-    return pl.pallas_call(
-        gather_kernel,
-        out_shape=jax.ShapeDtypeStruct((4, 256, WIDE), jnp.bfloat16),
-        in_specs=[pl.BlockSpec(memory_space=pltpu.VMEM)],
-        out_specs=pl.BlockSpec(memory_space=pltpu.VMEM),
-        scratch_shapes=[dma, dma, dma, dma((7,)), dma((7,)), dma((16,)), dma((16,)), dma((8,)), dma((8,))],
-        compiler_params=pltpu.CompilerParams(
-            collective_id=0, has_side_effects=True, vmem_limit_bytes=VMEM_LIMIT
-        ),
-        name="gather_weights",
-    )(packed)
 
 
 def reduce_kernel(
@@ -431,12 +296,34 @@
 
 
 STEPS = (0, 1, 3, 2)
-
-
-def expert_kernel(
-    rows_ref, cot_ref, inner_hbm, outer_hbm, y_ref, z_ref, inner_grad_hbm, outer_grad_hbm,
-    slots, cots, active, pre, inner, outer, part_y, part_z, straight_y, straight_z, relay_y, relay_z, joint_y, joint_z,
-    grad_buf, sized, load_sem, self_s, there_s, there_r, ring_s, ring_r, fold_s, fold_r, back_s, back_r, store_sem
+TALL = 1152
+
+
+def columns_of(n, width):
+    return pl.ds(pl.multiple_of(n * width, width), width)
+
+
+def mask_of(length_ref):
+    return (lax.broadcasted_iota(jnp.int32, (128, 1), 0) < length_ref[0]).astype(jnp.float32)
+
+
+def chosen_of(ids_ref):
+    lane = lax.broadcasted_iota(jnp.int32, (128, 128), 1)
+    return [lane == ids_ref[:, k : k + 1] for k in (0, 1)]
+
+
+def identity():
+    shape = (128, 128)
+    return (lax.broadcasted_iota(jnp.int32, shape, 0) == lax.broadcasted_iota(jnp.int32, shape, 1)).astype(jnp.bfloat16)
+
+
+def main_kernel(
+    frames_ref, length_ref, ids_ref, og_ref, conv_in_ref, router_ref, depthwise_ref, inner_hbm, outer_hbm,
+    out_ref, mixed_ref, value_ref, sig_ref, conv_ref, xhat_ref, notes_ref, gated_ref, taps_ref,
+    y_ref, z_ref, inner_grad_hbm, outer_grad_hbm,
+    own_ref, rows_buf, og_rows, slots, cots, scaled, active, pre, inner, outer, part_y, part_z, straight_y, straight_z,
+    relay_y, relay_z, joint_y, joint_z, grad_buf, sized, load_sem, core_s, core_r, own_sem, z_s, z_r, gring_s, gring_r,
+    tail_s, tail_r, self_s, there_s, there_r, ring_s, ring_r, fold_s, fold_r, back_s, back_r, store_sem
 ):
     x, y, z, c = place()
     f32, bf = jnp.float32, jnp.bfloat16
@@ -459,64 +346,274 @@
     lax.fori_loop(1, 64, hail, 0)
     for where in (to_right, to_left):
         pl.semaphore_signal(barrier, inc=1, device_id=where, device_id_type=MESH)
+
+    own_ref[:, 0:2048] = conv_in_ref[...]
+    own_ref[:, 2048:WIDE] = jnp.concatenate(
+        [router_ref[...].astype(f32), depthwise_ref[...].astype(f32), jnp.zeros((4, WIDE - 2112 - KERNEL), f32)], axis=1
+    ).astype(bf)
+    mask = mask_of(length_ref)
+    picks = chosen_of(ids_ref)
+    count = (jnp.where(picks[0] | picks[1], 1.0, 0.0) * mask).astype(bf)
+    shape = (128, 128)
+    below = (lax.broadcasted_iota(jnp.int32, shape, 1) < lax.broadcasted_iota(jnp.int32, shape, 0)).astype(bf)
+    before = jnp.dot(below, count, preferred_element_type=f32)
+    wide = lax.broadcasted_iota(jnp.int32, (128, 256), 1).astype(f32)
+    slot_of, spots = [], []
+    for k, pick in enumerate(picks):
+        position = jnp.sum(jnp.where(pick, before, 0.0), axis=1, keepdims=True)
+        kept = (position < 4.0) & (mask > 0.0)
+        slot = jnp.where(kept, ids_ref[:, k : k + 1].astype(f32) * 4.0 + position, -1.0)
+        slot_of.append(slot)
+        spots.append((wide == slot).astype(bf))
+    both = spots[0] + spots[1]
+    down = (((0,), (0,)), ((), ()))
+
+    def fill_og(n, carry):
+        cols = columns_of(n, 256)
+        og_rows[:, cols] = lax.dot_general(both, og_ref[:, cols], down, preferred_element_type=f32).astype(bf)
+        return carry
+
+    lax.fori_loop(0, 4, fill_og, 0)
     pl.semaphore_wait(barrier, 65)
 
     own4 = pl.multiple_of(4 * here, 4)
     line4 = pl.multiple_of(8 * z + 4 * c, 4)
-    kinds = ((rows_ref, slots), (cot_ref, cots))
-    selfs = []
-    for kind, (source, target) in enumerate(kinds):
-        copy = pltpu.make_async_copy(
-            source.at[pl.ds(own4, 4)], target.at[x, y, pl.ds(line4, 4)], self_s.at[kind]
-        )
-        copy.start()
-        selfs.append(copy)
-    for q, dy in enumerate(STEPS):
+    kinds = ((rows_buf, slots, TALL), (og_rows, cots, 1024))
+    selfs = {}
+    rings = {}
+
+    def source_y(q):
+        return (y + STEPS[q]) % 4
+
+    def depart(kind, q):
+        source, target, _ = kinds[kind]
+        dy = STEPS[q]
         yt = (y + 4 - dy) % 4
 
-        def there(i, carry, yt=yt, q=q):
+        def there(i, carry):
             zt, ct = (z + 4 + i // 2) % 8, (c + i) % 2
             et = yt * 16 + zt * 2 + ct
             rows = pl.ds(pl.multiple_of(4 * et, 4), 4)
-            for kind, (source, target) in enumerate(kinds):
-                remote(
-                    source.at[rows], target.at[x, y, pl.ds(line4, 4)], there_s.at[kind, q], there_r.at[kind, q], (x, et)
-                ).start()
+            remote(
+                source.at[rows], target.at[x, y, pl.ds(line4, 4)], there_s.at[kind, q], there_r.at[kind, q], (x, et)
+            ).start()
             return carry
 
         if dy == 0:
             lax.fori_loop(0, 8, there, 0)
             lax.fori_loop(9, 16, there, 0)
+            selfs[kind] = pltpu.make_async_copy(
+                source.at[pl.ds(own4, 4)], target.at[x, y, pl.ds(line4, 4)], self_s.at[kind]
+            )
+            selfs[kind].start()
         else:
             lax.fori_loop(0, 16, there, 0)
 
-    def source_y(q):
-        return (y + STEPS[q]) % 4
-
-    rings = {}
-
-    def arrive(q):
-        ys = source_y(q)
+    def bulk(kind, q):
+        return sized.at[pl.ds(0, 15 if STEPS[q] == 0 else 16), :, pl.ds(0, kinds[kind][2])]
+
+    def arrive(kind, q):
         if STEPS[q] == 0:
-            for copy in selfs:
-                copy.wait()
-        for kind, (_, target) in enumerate(kinds):
-            view = sized.at[pl.ds(0, 15 if STEPS[q] == 0 else 16)]
-            remote(view, view, there_s.at[kind, q], there_r.at[kind, q], to_right).wait_recv()
-            block = target.at[x, ys]
-            for side, where in ((0, to_right), (1, to_left)):
-                copy = remote(block, block, ring_s.at[kind, side, q], ring_r.at[kind, side, q], where)
-                copy.start()
-                rings[kind, side, q] = copy
-
-    def forward(q):
-        ys = source_y(q)
-        for kind, side, at, where in ((0, 0, left, to_right), (1, 1, right, to_left)):
+            selfs[kind].wait()
+        view = bulk(kind, q)
+        remote(view, view, there_s.at[kind, q], there_r.at[kind, q], to_right).wait_recv()
+        block = kinds[kind][1].at[x, source_y(q)]
+        for side, where in ((0, to_right), (1, to_left)):
+            copy = remote(block, block, ring_s.at[kind, side, q], ring_r.at[kind, side, q], where)
+            copy.start()
+            rings[kind, side, q] = copy
+
+    def forward(kind, q):
+        for side, at, where in ((0, left, to_right), (1, right, to_left)):
             rings[kind, side, q].wait_recv()
-            block = kinds[kind][1].at[at, ys]
-            copy = remote(block, block, ring_s.at[kind, 2, q], ring_r.at[kind, 2, q], where)
+            block = kinds[kind][1].at[at, source_y(q), pl.ds(32 * side, 32)]
+            copy = remote(block, block, ring_s.at[kind, 2 + side, q], ring_r.at[kind, 2 + side, q], where)
             copy.start()
-            rings[kind, 2, q] = copy
+            rings[kind, 2 + side, q] = copy
+
+    partner = spot(x, y, z, 1 - c)
+    mine = pl.multiple_of(c * HALF, 128)
+    other = pl.multiple_of((1 - c) * HALF, 128)
+    row = pl.multiple_of(y * 64 + z * 8, 8)
+    row4 = pl.multiple_of(row + 4 * c, 4)
+    swap = remote(
+        own_ref.at[:, pl.ds(other, HALF)],
+        out_ref.at[x, pl.ds(row4, 4), pl.ds(other, HALF)],
+        core_s,
+        core_r,
+        partner,
+    )
+    swap.start()
+    keep = pltpu.make_async_copy(
+        own_ref.at[:, pl.ds(mine, HALF)], out_ref.at[x, pl.ds(row4, 4), pl.ds(mine, HALF)], own_sem
+    )
+    keep.start()
+    depart(1, 0)
+    keep.wait()
+    swap.wait()
+    copies = []
+    for dz in (4, 3, 5, 2, 6, 1, 7):
+        block = out_ref.at[x, pl.ds(row, 8), pl.ds(mine, HALF)]
+        copy = remote(block, block, z_s.at[dz - 1], z_r.at[dz - 1], spot(x, y, (z + dz) % 8, c))
+        copy.start()
+        copies.append(copy)
+    depart(1, 1)
+    xhat, inv_scale = normalize(frames_ref[...].astype(f32))
+    xhat_ref[...] = xhat
+    zeros = jnp.zeros((16, 1024), f32)
+    gated_ref[0:16, :] = zeros
+    gated_ref[144:160, :] = zeros
+    for copy in copies:
+        copy.wait()
+
+    first = pl.multiple_of(mine, 128)
+    second = pl.multiple_of(mine + SPLIT, 128)
+    yrow = pl.multiple_of(y * 64, 64)
+
+    def block_of(colour, level, index, part):
+        cols = pl.ds(first, SPLIT) if colour == 0 else pl.ds(second, HALF - SPLIT)
+        if level == 0:
+            height = 64 if part is None else 32
+            offset = 0 if part is None else part * 32
+            if colour == 0:
+                return out_ref.at[x, pl.ds(pl.multiple_of(index * 64 + offset, 32), height), cols]
+            return out_ref.at[index, pl.ds(pl.multiple_of(yrow + offset, 32), height), cols]
+        if colour == 0:
+            height = 256 if part is None else 128
+            offset = 0 if part is None else part * 128
+            return out_ref.at[index, pl.ds(offset, height), cols]
+        height = 64 if part is None else 32
+        offset = 0 if part is None else part * 32
+        return out_ref.at[:, pl.ds(pl.multiple_of(index * 64 + offset, 32), height), cols]
+
+    def whereto(colour, level, step):
+        if (colour + level) % 2 == 0:
+            return spot(x, (y + step) % 4, z, c)
+        return spot((x + step) % 4, y, z, c)
+
+    def position(colour, level):
+        return y if (colour + level) % 2 == 0 else x
+
+    def opened(colour, level):
+        at = position(colour, level)
+        block = block_of(colour, level, at, None)
+        base = (colour * 2 + level) * 4
+        right = remote(block, block, gring_s.at[base], gring_r.at[base], whereto(colour, level, 1))
+        left = remote(block, block, gring_s.at[base + 1], gring_r.at[base + 1], whereto(colour, level, 3))
+        right.start()
+        left.start()
+        return right, left
+
+    def passed(colour, level, pair, tell):
+        at = position(colour, level)
+        base = (colour * 2 + level) * 4
+        right, left = pair
+        right.wait_recv()
+        block = block_of(colour, level, (at + 3) % 4, 0)
+        on_right = remote(block, block, gring_s.at[base + 2], gring_r.at[base + 2], whereto(colour, level, 1))
+        on_right.start()
+        tell((at + 3) % 4, 1)
+        left.wait_recv()
+        block = block_of(colour, level, (at + 1) % 4, 1)
+        on_left = remote(block, block, gring_s.at[base + 3], gring_r.at[base + 3], whereto(colour, level, 3))
+        on_left.start()
+        tell((at + 1) % 4, 2)
+        return on_right, on_left
+
+    def closed(colour, level, pair, onward, tell):
+        at = position(colour, level)
+        for copy in onward:
+            copy.wait_recv()
+        tell((at + 2) % 4, 3)
+        for copy in pair + onward:
+            copy.wait_send()
+
+    silent = lambda index, slot: None
+    low = [opened(colour, 0) for colour in (0, 1)]
+    arrive(1, 0)
+    low_on = [passed(colour, 0, low[colour], silent) for colour in (0, 1)]
+    depart(1, 2)
+    for colour in (0, 1):
+        closed(colour, 0, low[colour], low_on[colour], silent)
+    tails = []
+
+    def teller(colour):
+        def tell(index, slot):
+            block = block_of(colour, 1, index, None)
+            at = colour * 4 + slot
+            copy = remote(block, block, tail_s.at[at], tail_r.at[at], partner)
+            copy.start()
+            tails.append(copy)
+
+        return tell
+
+    high = [opened(colour, 1) for colour in (0, 1)]
+    for colour in (0, 1):
+        teller(colour)(position(colour, 1), 0)
+    depart(1, 3)
+    arrive(1, 1)
+    high_on = [passed(colour, 1, high[colour], teller(colour)) for colour in (0, 1)]
+    forward(1, 0)
+    for colour in (0, 1):
+        closed(colour, 1, high[colour], high_on[colour], teller(colour))
+    arrive(1, 2)
+    for copy in tails:
+        copy.wait()
+    forward(1, 1)
+    arrive(1, 3)
+
+    normed = xhat_ref[...].astype(bf)
+
+    def point(n, carry):
+        cols = columns_of(n, 256)
+        value = jnp.dot(normed, out_ref[:, :, cols].reshape(1024, 256), preferred_element_type=f32)
+        gate = jnp.dot(normed, out_ref[:, :, columns_of(n + 4, 256)].reshape(1024, 256), preferred_element_type=f32)
+        sig = jax.nn.sigmoid(gate)
+        value_ref[:, cols] = value
+        sig_ref[:, cols] = sig
+        gated_ref[16:144, cols] = value * sig * mask
+        return carry
+
+    lax.fori_loop(0, 4, point, 0)
+    small = out_ref[:, :, 2048:2176].reshape(1024, 128)
+    taps_ref[...] = lax.dot_general(identity(), small, (((1,), (1,)), ((), ())), preferred_element_type=f32)
+    forward(1, 2)
+
+    def depth(n, carry):
+        cols = columns_of(n, 128)
+        total = jnp.zeros((128, 128), f32)
+        for k in range(KERNEL):
+            total = total + taps_ref[64 + k : 65 + k, cols] * gated_ref[k + 1 : k + 129, cols]
+        conv_ref[:, cols] = total
+        mixed_ref[:, cols] = (frames_ref[:, cols].astype(f32) + swish_of(total) * mask).astype(bf)
+        return carry
+
+    lax.fori_loop(0, 8, depth, 0)
+    logits = jnp.dot(mixed_ref[...], small, preferred_element_type=f32)
+    scores = [jax.nn.sigmoid(jnp.sum(jnp.where(pick, logits, 0.0), axis=1, keepdims=True)) for pick in picks]
+    score_sum = scores[0] + scores[1]
+    weights = [score / score_sum for score in scores]
+    lane = lax.broadcasted_iota(jnp.int32, shape, 1)
+    notes = jnp.zeros(shape, f32)
+    for i, column in enumerate(weights + scores + [score_sum] + slot_of + [inv_scale]):
+        notes = jnp.where(lane == i, column, notes)
+    notes_ref[...] = notes
+
+    def fill(n, carry):
+        cols = columns_of(n, 256)
+        rows_buf[:, cols] = lax.dot_general(both, mixed_ref[:, cols], down, preferred_element_type=f32).astype(bf)
+        return carry
+
+    lax.fori_loop(0, 4, fill, 0)
+    total = jnp.zeros((256, 128), f32)
+    for k in (0, 1):
+        upper = weights[k].astype(bf).astype(f32)
+        parts = jnp.where(lane == 0, upper, jnp.where(lane == 1, weights[k] - upper, 0.0)).astype(bf)
+        total = total + lax.dot_general(spots[k], parts, down, preferred_element_type=f32)
+    rows_buf[:, 1024:TALL] = total.astype(bf)
+    for q in range(4):
+        depart(0, q)
+    forward(1, 3)
 
     folds = {}
 
@@ -527,16 +624,23 @@
 
     def compute(q):
         ys = source_y(q)
-        rings[0, 1, q].wait_recv()
-        rings[1, 0, q].wait_recv()
-        rings[0, 2, q].wait_recv()
-        rings[1, 2, q].wait_recv()
+        for kind in (1, 0):
+            for side in (2, 3):
+                rings[kind, side, q].wait_recv()
+
+        def scale(n, carry):
+            parts = slots[n, ys, :, 1024:TALL].astype(f32)
+            weight = parts[:, 0:1] + parts[:, 1:2]
+            scaled[n, ys] = (cots[n, ys].astype(f32) * weight).astype(bf)
+            return carry
+
+        lax.fori_loop(0, 4, scale, 0)
 
         def first(n, carry):
             cols = pl.ds(pl.multiple_of(n * 256, 256), 256)
-            hidden = jnp.dot(slots[:, ys].reshape(256, 1024), inner[:, cols], preferred_element_type=f32)
+            hidden = jnp.dot(slots[:, ys, :, 0:1024].reshape(256, 1024), inner[:, cols], preferred_element_type=f32)
             act_grad = lax.dot_general(
-                cots[:, ys].reshape(256, 1024), outer[cols, :], (((1,), (1,)), ((), ())), preferred_element_type=f32
+                scaled[:, ys].reshape(256, 1024), outer[cols, :], (((1,), (1,)), ((), ())), preferred_element_type=f32
             )
             sig = jax.nn.sigmoid(hidden)
             active[:, ys, :, cols] = (hidden * sig).astype(bf).reshape(4, 64, 256)
@@ -545,7 +649,6 @@
             return carry
 
         lax.fori_loop(0, 4, first, 0)
-
         def second(n, carry):
             cols = pl.ds(pl.multiple_of(n * 256, 256), 256)
             out = jnp.dot(active[:, ys].reshape(256, 1024), outer[:, cols], preferred_element_type=f32)
@@ -594,7 +697,7 @@
                     source.at[q, x, pl.ds(line4, 4)], target.at[pl.ds(own4, 4)], self_s.at[2 + kind]
                 )
                 copy.start()
-                selfs.append(copy)
+                selfs[2 + kind] = copy
         else:
             lax.fori_loop(0, 16, back, 0)
 
@@ -617,193 +720,77 @@
         copy.start()
         stores.append(copy)
 
-    arrive(0)
     for load in loads:
         load.wait()
-    arrive(1)
-    forward(0)
-    arrive(2)
-    forward(1)
+    arrive(0, 0)
+    arrive(0, 1)
+    forward(0, 0)
+    arrive(0, 2)
+    forward(0, 1)
     compute(0)
-    arrive(3)
-    forward(2)
+    arrive(0, 3)
+    forward(0, 2)
     compute(1)
     relay(0)
-    forward(3)
+    forward(0, 3)
     compute(2)
     relay(1)
     deliver(0)
     compute(3)
     relay(2)
     deliver(1)
-    weight_grad(1, active, cots, outer_grad_hbm)
+    weight_grad(1, active, scaled, outer_grad_hbm)
     relay(3)
     deliver(2)
     weight_grad(0, slots, pre, inner_grad_hbm)
     deliver(3)
     for kind in (0, 1):
         for q in range(4):
-            view = sized.at[pl.ds(0, 15 if STEPS[q] == 0 else 16)]
+            view = bulk(kind, q)
             remote(view, view, there_s.at[kind, q], there_r.at[kind, q], to_right).wait_send()
-    for copy in rings.values():
-        copy.wait_send()
-    for copy in folds.values():
+    for copy in list(rings.values()) + list(folds.values()):
         copy.wait_send()
     for kind in (0, 1):
-        view = sized.at[pl.ds(0, 63)]
+        view = sized.at[pl.ds(0, 63), :, pl.ds(0, 1024)]
         remote(view, view, back_s.at[kind], back_r.at[kind], to_right).wait()
-    for copy in selfs[2:] + stores:
+    for copy in [selfs[2], selfs[3]] + stores:
         copy.wait()
 
 
-def expert_pass(rows, cot, inner, outer):
-    dma, bf = pltpu.SemaphoreType.DMA, jnp.bfloat16
+def main_pass(frames, lengths, ids, og, conv_in, router, depthwise, inner, outer):
+    dma, bf, f32 = pltpu.SemaphoreType.DMA, jnp.bfloat16, jnp.float32
     block = lambda *lead: pltpu.VMEM(lead + (64, 1024), bf)
-    whole = jax.ShapeDtypeStruct((1024, 1024), bf)
-    slot = jax.ShapeDtypeStruct((256, 1024), bf)
+    shape = lambda *args: jax.ShapeDtypeStruct(*args)
     vmem, anywhere = pl.BlockSpec(memory_space=pltpu.VMEM), pl.BlockSpec(memory_space=pl.ANY)
     return pl.pallas_call(
-        expert_kernel,
-        out_shape=(slot, slot, whole, whole),
-        in_specs=[vmem, vmem, anywhere, anywhere],
-        out_specs=(vmem, vmem, anywhere, anywhere),
-        scratch_shapes=[block(4, 4)] * 4
+        main_kernel,
+        out_shape=(
+            shape((4, 256, WIDE), bf), shape((128, 1024), bf), shape((128, 1024), f32), shape((128, 1024), f32),
+            shape((128, 1024), f32), shape((128, 1024), f32), shape((128, 128), f32), shape((160, 1024), f32),
+            shape((128, 1024), f32), shape((256, 1024), bf), shape((256, 1024), bf), shape((1024, 1024), bf),
+            shape((1024, 1024), bf),
+        ),
+        in_specs=[vmem, pl.BlockSpec(memory_space=pltpu.SMEM)] + [vmem] * 5 + [anywhere] * 2,
+        out_specs=(vmem,) * 11 + (anywhere,) * 2,
+        scratch_shapes=[
+            pltpu.VMEM((4, WIDE), bf), pltpu.VMEM((256, TALL), bf), pltpu.VMEM((256, 1024), bf),
+            pltpu.VMEM((4, 4, 64, TALL), bf),
+        ]
+        + [block(4, 4)] * 4
         + [pltpu.VMEM((1024, 1024), bf)] * 2
         + [block(4, 4)] * 2
         + [block(4)] * 6
-        + [pltpu.VMEM((2, 1024, 1024), bf), pltpu.VMEM((63, 4, 1024), bf)]
+        + [pltpu.VMEM((2, 1024, 1024), bf), pltpu.VMEM((63, 4, TALL), bf)]
         + [
-            dma((2,)),
-            dma((4,)),
-            dma((2, 4)),
-            dma((2, 4)),
-            dma((2, 3, 4)),
-            dma((2, 3, 4)),
-            dma((6, 4)),
-            dma((6, 4)),
-            dma((2,)),
-            dma((2,)),
-            dma((2,)),
+            dma((2,)), dma, dma, dma, dma((7,)), dma((7,)), dma((16,)), dma((16,)), dma((8,)), dma((8,)),
+            dma((4,)), dma((2, 4)), dma((2, 4)), dma((2, 4, 4)), dma((2, 4, 4)), dma((6, 4)), dma((6, 4)), dma((2,)),
+            dma((2,)), dma((2,)),
         ],
         compiler_params=pltpu.CompilerParams(
             collective_id=2, has_side_effects=True, vmem_limit_bytes=VMEM_LIMIT
         ),
-        name="expert_pass",
-    )(rows, cot, inner, outer)
-
-
-def columns_of(n, width):
-    return pl.ds(pl.multiple_of(n * width, width), width)
-
-
-def mask_of(length_ref):
-    return (lax.broadcasted_iota(jnp.int32, (128, 1), 0) < length_ref[0]).astype(jnp.float32)
-
-
-def chosen_of(ids_ref):
-    lane = lax.broadcasted_iota(jnp.int32, (128, 128), 1)
-    return [lane == ids_ref[:, k : k + 1] for k in (0, 1)]
-
-
-def identity():
-    shape = (128, 128)
-    return (lax.broadcasted_iota(jnp.int32, shape, 0) == lax.broadcasted_iota(jnp.int32, shape, 1)).astype(jnp.bfloat16)
-
-
-def front_kernel(
-    frames_ref, length_ref, ids_ref, og_ref, full_ref, rows_ref, cot_ref, mixed_ref, value_ref, sig_ref, conv_ref,
-    xhat_ref, notes_ref, gated_ref, taps_ref
-):
-    f32, bf = jnp.float32, jnp.bfloat16
-    mask = mask_of(length_ref)
-    xhat, inv_scale = normalize(frames_ref[...].astype(f32))
-    xhat_ref[...] = xhat
-    normed = xhat.astype(bf)
-    zeros = jnp.zeros((16, 1024), f32)
-    gated_ref[0:16, :] = zeros
-    gated_ref[144:160, :] = zeros
-
-    def point(n, carry):
-        cols = columns_of(n, 256)
-        value = jnp.dot(normed, full_ref[:, :, cols].reshape(1024, 256), preferred_element_type=f32)
-        gate = jnp.dot(normed, full_ref[:, :, columns_of(n + 4, 256)].reshape(1024, 256), preferred_element_type=f32)
-        sig = jax.nn.sigmoid(gate)
-        value_ref[:, cols] = value
-        sig_ref[:, cols] = sig
-        gated_ref[16:144, cols] = value * sig * mask
-        return carry
-
-    lax.fori_loop(0, 4, point, 0)
-    small = full_ref[:, :, 2048:2176].reshape(1024, 128)
-    taps_ref[...] = lax.dot_general(identity(), small, (((1,), (1,)), ((), ())), preferred_element_type=f32)
-
-    def depth(n, carry):
-        cols = columns_of(n, 128)
-        total = jnp.zeros((128, 128), f32)
-        for k in range(KERNEL):
-            total = total + taps_ref[64 + k : 65 + k, cols] * gated_ref[k + 1 : k + 129, cols]
-        conv_ref[:, cols] = total
-        mixed_ref[:, cols] = (frames_ref[:, cols].astype(f32) + swish_of(total) * mask).astype(bf)
-        return carry
-
-    lax.fori_loop(0, 8, depth, 0)
-    mixed = mixed_ref[...]
-    logits = jnp.dot(mixed, small, preferred_element_type=f32)
-    picks = chosen_of(ids_ref)
-    scores = [jax.nn.sigmoid(jnp.sum(jnp.where(pick, logits, 0.0), axis=1, keepdims=True)) for pick in picks]
-    score_sum = scores[0] + scores[1]
-    weights = [score / score_sum for score in scores]
-    count = (jnp.where(picks[0] | picks[1], 1.0, 0.0) * mask).astype(bf)
-    shape = (128, 128)
-    below = (lax.broadcasted_iota(jnp.int32, shape, 1) < lax.broadcasted_iota(jnp.int32, shape, 0)).astype(bf)
-    before = jnp.dot(below, count, preferred_element_type=f32)
-    wide = lax.broadcasted_iota(jnp.int32, (128, 256), 1).astype(f32)
-    slots, spots = [], []
-    for k, pick in enumerate(picks):
-        position = jnp.sum(jnp.where(pick, before, 0.0), axis=1, keepdims=True)
-        kept = (position < 4.0) & (mask > 0.0)
-        slot = jnp.where(kept, ids_ref[:, k : k + 1].astype(f32) * 4.0 + position, -1.0)
-        slots.append(slot)
-        spots.append((wide == slot).astype(bf))
-    lane = lax.broadcasted_iota(jnp.int32, shape, 1)
-    notes = jnp.zeros(shape, f32)
-    for i, column in enumerate(weights + scores + [score_sum] + slots + [inv_scale]):
-        notes = jnp.where(lane == i, column, notes)
-    notes_ref[...] = notes
-    both = spots[0] + spots[1]
-
-    def fill(n, carry):
-        cols = columns_of(n, 256)
-        down = (((0,), (0,)), ((), ()))
-        rows_ref[:, cols] = lax.dot_general(both, mixed_ref[:, cols], down, preferred_element_type=f32).astype(bf)
-        og = og_ref[:, cols].astype(f32)
-        total = jnp.zeros((256, 256), f32)
-        for k in (0, 1):
-            total = total + lax.dot_general(
-                spots[k], (weights[k] * og).astype(bf), down, preferred_element_type=f32
-            )
-        cot_ref[:, cols] = total.astype(bf)
-        return carry
-
-    lax.fori_loop(0, 4, fill, 0)
-
-
-def front(frames, lengths, ids, og, full):
-    bf, f32 = jnp.bfloat16, jnp.float32
-    vmem = pl.BlockSpec(memory_space=pltpu.VMEM)
-    shape = lambda *args: jax.ShapeDtypeStruct(*args)
-    return pl.pallas_call(
-        front_kernel,
-        out_shape=(
-            shape((256, 1024), bf), shape((256, 1024), bf), shape((128, 1024), bf), shape((128, 1024), f32),
-            shape((128, 1024), f32), shape((128, 1024), f32), shape((128, 1024), f32), shape((128, 128), f32),
-            shape((160, 1024), f32), shape((128, 1024), f32),
-        ),
-        in_specs=[vmem, pl.BlockSpec(memory_space=pltpu.SMEM), vmem, vmem, vmem],
-        out_specs=(vmem,) * 10,
-        compiler_params=pltpu.CompilerParams(vmem_limit_bytes=VMEM_LIMIT),
-        name="front",
-    )(frames, lengths, ids, og, full)
+        name="main_pass",
+    )(frames, lengths, ids, og, conv_in, router, depthwise, inner, outer)
 
 
 def back_kernel(
@@ -942,16 +929,11 @@
 
 
 def per_device(frames, lengths, expert_ids, conv_in, depthwise, router, w_in, w_out, out_grad):
-    width = frames.shape[1]
-    experts = router.shape[1]
-    packed = jnp.concatenate(
-        [conv_in, router, jnp.pad(depthwise, ((0, 0), (0, WIDE - 2 * width - experts - KERNEL)))], axis=1
+    full, *saved, y, z, inner, outer = main_pass(
+        frames, lengths, expert_ids, out_grad, conv_in, router, depthwise, w_in[0], w_out[0]
     )
-    full = gather_weights(packed)
-    rows, cot, *saved = front(frames, lengths, expert_ids, out_grad, full)
-    expert_rows, back_rows, inner, outer = expert_pass(rows, cot, w_in[0], w_out[0])
     layer_out, frames_grad, part, w_in_grad, w_out_grad = backward(
-        expert_rows, back_rows, out_grad, saved, lengths, expert_ids, full, inner, outer
+        y, z, out_grad, saved, lengths, expert_ids, full, inner, outer
     )
     conv_in_grad, depthwise_grad, router_grad = reduce_grads(part)
     return (

time: 221 us -> 203 us (0.919)
  Pallas kernels: 212 us -> 196 us
    pallas_call x3 -> x1, Pallas kernels: 154 us -> 138 us  [main_pass(): pl.pallas_call(main_kernel, out_shape=(shape((4, 256, WIDE), bf), shape((...]
where the time goes in v2:
time: 203 us
  Pallas kernels  196 us (97%)
  local copies, waits for them, and re-layouts  5.26 us (3%)
    pallas_call x1, Pallas kernels, main_pass(): pl.pallas_call(main_kernel, out_shape=(shape((4, 256, WIDE), bf), shape((...  138 us
    pallas_call x1, Pallas kernels, reduce_grads(): pl.pallas_call(reduce_kernel, out_shape=tuple((jax.ShapeDtypeStruct((4, w...  39.1 us
    pallas_call x1, Pallas kernels, backward(): pl.pallas_call(back_kernel, out_shape=(shape((128, 1024), bf), shape((128...  19.6 us
    unnamed x4, local copies, waits for them, and re-layouts  5.26 us

profile of v2, /device:TPU:1, one launch (start us, length us, event | category | flops | bytes accessed | tf_op | source)
XLA Modules:
  0.0 203.0 jit_solution(14525109439603156769)
XLA Ops:
  1.3 1.4 copy.16.ids_ref
  2.7 137.8 %main_pass.1 = (bf16[4,256,2304]{2,1,0:T(8,128)(2,1)}, bf16[128,1024]{1,0:T(8,128)(2,1)}, f32[128,1024]{1,0:T(8,128)}, f32[128,1024]{1,0:T(8,128)}, f32[128,1024...) custom-call(bf16[128,1024]{1,0:T(8,128)(2,1)} %frames_ref.1, ...), custom_call_target="tpu_custom_call" | custom-call | tf_op jit(solution)/shard_map/main_pass/pallas_call | solution.py:765
  140.5 19.6 %backward.1 = (bf16[128,1024]{1,0:T(8,128)(2,1)}, bf16[128,1024]{1,0:T(8,128)(2,1)}, bf16[4,256,2304]{2,1,0:T(8,128)(2,1)}, bf16[1024,1024]{1,0:T(8,128)(2,1)}, bf16[1024,1024]{1,0:T(8,128)(2,1)}) custom-call(bf16[256,1024]{1,0:T(8,128)(2,1)} %get-tuple-element.28.y_ref, bf16[256,1024]{1,0:T(8,128)(2,1)} %get-tuple-element.29.z_ref, ...), custom_call_target="tpu_custom_call" | custom-call | tf_op jit(solution)/shard_map/backward/pallas_call | solution.py:911
  160.0 39.1 %reduce_grads.1 = (f32[4,2048]{1,0:T(4,128)}, f32[4,31]{1,0:T(4,128)}, f32[4,64]{1,0:T(4,128)}) custom-call(bf16[4,256,2304]{2,1,0:T(8,128)(2,1)} %get-tuple-element.43.part_ref), custom_call_target="tpu_custom_call" | custom-call | tf_op jit(solution)/shard_map/reduce_grads/pallas_call | solution.py:265
  199.1 1.4 copy.22
  200.5 1.2 copy.23
  201.7 1.2 copy.24

commit v3 on v2

v3 whole, which is shorter than its diff:
```python
import jax
import jax.numpy as jnp
from jax import lax
from jax.experimental import pallas as pl
from jax.experimental.pallas import tpu as pltpu
from jax.sharding import PartitionSpec as P

KERNEL = 31
EPSILON = 1e-05


def swish_of(values):
    return values * jax.nn.sigmoid(values)


def swish_slope(values):
    sigmoid_v = jax.nn.sigmoid(values)
    return sigmoid_v * (1.0 + values * (1.0 - sigmoid_v))


def normalize(values):
    center = values - jnp.mean(values, axis=-1, keepdims=True)
    inv_scale = lax.rsqrt(jnp.mean(center * center, axis=-1, keepdims=True) + EPSILON)
    return (center * inv_scale, inv_scale)


MESH = pl.DeviceIdType.MESH
HALF = 1152
WIDE = 2 * HALF
SPLIT = 640
VMEM_LIMIT = 60 * 1024 * 1024


def place():
    x = lax.axis_index("dp")
    e = lax.axis_index("expert")
    return x, e // 16, (e // 2) % 8, e % 2


def spot(x, y, z, c):
    return (x, y * 16 + z * 2 + c)


def remote(src, dst, send, recv, where):
    return pltpu.make_async_remote_copy(
        src_ref=src, dst_ref=dst, send_sem=send, recv_sem=recv, device_id=where, device_id_type=MESH
    )


STEPS = (0, 1, 3, 2)
TALL = 1152


def columns_of(n, width):
    return pl.ds(pl.multiple_of(n * width, width), width)


def mask_of(length_ref):
    return (lax.broadcasted_iota(jnp.int32, (128, 1), 0) < length_ref[0]).astype(jnp.float32)


def chosen_of(ids_ref):
    lane = lax.broadcasted_iota(jnp.int32, (128, 128), 1)
    return [lane == ids_ref[:, k : k + 1] for k in (0, 1)]


def identity():
    shape = (128, 128)
    return (lax.broadcasted_iota(jnp.int32, shape, 0) == lax.broadcasted_iota(jnp.int32, shape, 1)).astype(jnp.bfloat16)


def layer_kernel(
    frames_ref, length_ref, ids_ref, og_ref, conv_in_ref, router_ref, depthwise_ref, inner_hbm, outer_hbm,
    layer_ref, frames_grad_ref, out_ref, depth_ref, router_grad_ref, inner_grad_hbm, outer_grad_hbm,
    full_ref, mixed_ref, value_ref, sig_ref, conv_ref, xhat_ref, gated_ref, taps_ref, y_ref, z_ref,
    own_ref, rows_buf, og_rows, slots, cots, scaled, active, pre, inner, outer, part_y, part_z, straight_y, straight_z,
    relay_y, relay_z, joint_y, joint_z, grad_buf, sized, mg_buf, cg_buf, tg_buf, pc_buf, turned, ng_buf,
    part_ref, swap_buf, half_buf, far_buf, near_buf, mid_buf, mid_far, mid_near, z_src, z_buf, last_src, last_buf,
    load_sem, core_s, core_r, own_sem, z_s, z_r, gring_s, gring_r, tail_s, tail_r, self_s, there_s, there_r, ring_s,
    ring_r, fold_s, fold_r, back_s, back_r, store_sem, swap_s, swap_r, rring_s, rring_r, rz_s, rz_r, last_s, last_r
):
    x, y, z, c = place()
    f32, bf = jnp.float32, jnp.bfloat16
    here = y * 16 + z * 2 + c
    right, left, far = (x + 1) % 4, (x + 3) % 4, (x + 2) % 4
    to_right, to_left = spot(right, y, z, c), spot(left, y, z, c)
    loads = [
        pltpu.make_async_copy(inner_hbm, inner, load_sem.at[0]),
        pltpu.make_async_copy(outer_hbm, outer, load_sem.at[1]),
    ]
    for load in loads:
        load.start()

    barrier = pltpu.get_barrier_semaphore()

    def hail(i, carry):
        pl.semaphore_signal(barrier, inc=1, device_id=(x, (here + i) % 64), device_id_type=MESH)
        return carry

    lax.fori_loop(1, 64, hail, 0)
    for where in (to_right, to_left):
        pl.semaphore_signal(barrier, inc=1, device_id=where, device_id_type=MESH)

    own_ref[:, 0:2048] = conv_in_ref[...]
    own_ref[:, 2048:WIDE] = jnp.concatenate(
        [router_ref[...].astype(f32), depthwise_ref[...].astype(f32), jnp.zeros((4, WIDE - 2112 - KERNEL), f32)], axis=1
    ).astype(bf)
    mask = mask_of(length_ref)
    picks = chosen_of(ids_ref)
    count = (jnp.where(picks[0] | picks[1], 1.0, 0.0) * mask).astype(bf)
    shape = (128, 128)
    below = (lax.broadcasted_iota(jnp.int32, shape, 1) < lax.broadcasted_iota(jnp.int32, shape, 0)).astype(bf)
    before = jnp.dot(below, count, preferred_element_type=f32)
    wide = lax.broadcasted_iota(jnp.int32, (128, 256), 1).astype(f32)
    slot_of, spots = [], []
    for k, pick in enumerate(picks):
        position = jnp.sum(jnp.where(pick, before, 0.0), axis=1, keepdims=True)
        kept = (position < 4.0) & (mask > 0.0)
        slot = jnp.where(kept, ids_ref[:, k : k + 1].astype(f32) * 4.0 + position, -1.0)
        slot_of.append(slot)
        spots.append((wide == slot).astype(bf))
    both = spots[0] + spots[1]
    down = (((0,), (0,)), ((), ()))

    def fill_og(n, carry):
        cols = columns_of(n, 256)
        og_rows[:, cols] = lax.dot_general(both, og_ref[:, cols], down, preferred_element_type=f32).astype(bf)
        return carry

    lax.fori_loop(0, 4, fill_og, 0)
    pl.semaphore_wait(barrier, 65)

    own4 = pl.multiple_of(4 * here, 4)
    line4 = pl.multiple_of(8 * z + 4 * c, 4)
    kinds = ((rows_buf, slots, TALL), (og_rows, cots, 1024))
    selfs = {}
    rings = {}

    def source_y(q):
        return (y + STEPS[q]) % 4

    def depart(kind, q):
        source, target, _ = kinds[kind]
        dy = STEPS[q]
        yt = (y + 4 - dy) % 4

        def there(i, carry):
            zt, ct = (z + 4 + i // 2) % 8, (c + i) % 2
            et = yt * 16 + zt * 2 + ct
            rows = pl.ds(pl.multiple_of(4 * et, 4), 4)
            remote(
                source.at[rows], target.at[x, y, pl.ds(line4, 4)], there_s.at[kind, q], there_r.at[kind, q], (x, et)
            ).start()
            return carry

        if dy == 0:
            lax.fori_loop(0, 8, there, 0)
            lax.fori_loop(9, 16, there, 0)
            selfs[kind] = pltpu.make_async_copy(
                source.at[pl.ds(own4, 4)], target.at[x, y, pl.ds(line4, 4)], self_s.at[kind]
            )
            selfs[kind].start()
        else:
            lax.fori_loop(0, 16, there, 0)

    def bulk(kind, q):
        return sized.at[pl.ds(0, 15 if STEPS[q] == 0 else 16), :, pl.ds(0, kinds[kind][2])]

    def arrive(kind, q):
        if STEPS[q] == 0:
            selfs[kind].wait()
        view = bulk(kind, q)
        remote(view, view, there_s.at[kind, q], there_r.at[kind, q], to_right).wait_recv()
        block = kinds[kind][1].at[x, source_y(q)]
        for side, where in ((0, to_right), (1, to_left)):
            copy = remote(block, block, ring_s.at[kind, side, q], ring_r.at[kind, side, q], where)
            copy.start()
            rings[kind, side, q] = copy

    def forward(kind, q):
        for side, at, where in ((0, left, to_right), (1, right, to_left)):
            rings[kind, side, q].wait_recv()
            block = kinds[kind][1].at[at, source_y(q), pl.ds(32 * side, 32)]
            copy = remote(block, block, ring_s.at[kind, 2 + side, q], ring_r.at[kind, 2 + side, q], where)
            copy.start()
            rings[kind, 2 + side, q] = copy

    partner = spot(x, y, z, 1 - c)
    mine = pl.multiple_of(c * HALF, 128)
    other = pl.multiple_of((1 - c) * HALF, 128)
    row = pl.multiple_of(y * 64 + z * 8, 8)
    row4 = pl.multiple_of(row + 4 * c, 4)
    swap = remote(
        own_ref.at[:, pl.ds(other, HALF)],
        full_ref.at[x, pl.ds(row4, 4), pl.ds(other, HALF)],
        core_s,
        core_r,
        partner,
    )
    swap.start()
    keep = pltpu.make_async_copy(
        own_ref.at[:, pl.ds(mine, HALF)], full_ref.at[x, pl.ds(row4, 4), pl.ds(mine, HALF)], own_sem
    )
    keep.start()
    depart(1, 0)
    keep.wait()
    swap.wait()
    copies = []
    for dz in (4, 3, 5, 2, 6, 1, 7):
        block = full_ref.at[x, pl.ds(row, 8), pl.ds(mine, HALF)]
        copy = remote(block, block, z_s.at[dz - 1], z_r.at[dz - 1], spot(x, y, (z + dz) % 8, c))
        copy.start()
        copies.append(copy)
    depart(1, 1)
    xhat, inv_scale = normalize(frames_ref[...].astype(f32))
    xhat_ref[...] = xhat
    zeros = jnp.zeros((16, 1024), f32)
    gated_ref[0:16, :] = zeros
    gated_ref[144:160, :] = zeros
    cg_buf[0:16, :] = zeros
    cg_buf[144:160, :] = zeros
    tg_buf[...] = jnp.zeros((128, 1024), f32)
    part_ref[:, :, 2176:2304] = jnp.zeros((4, 256, 128), bf)
    for copy in copies:
        copy.wait()

    first = pl.multiple_of(mine, 128)
    second = pl.multiple_of(mine + SPLIT, 128)
    yrow = pl.multiple_of(y * 64, 64)

    def block_of(colour, level, index, part):
        cols = pl.ds(first, SPLIT) if colour == 0 else pl.ds(second, HALF - SPLIT)
        if level == 0:
            height = 64 if part is None else 32
            offset = 0 if part is None else part * 32
            if colour == 0:
                return full_ref.at[x, pl.ds(pl.multiple_of(index * 64 + offset, 32), height), cols]
            return full_ref.at[index, pl.ds(pl.multiple_of(yrow + offset, 32), height), cols]
        if colour == 0:
            height = 256 if part is None else 128
            offset = 0 if part is None else part * 128
            return full_ref.at[index, pl.ds(offset, height), cols]
        height = 64 if part is None else 32
        offset = 0 if part is None else part * 32
        return full_ref.at[:, pl.ds(pl.multiple_of(index * 64 + offset, 32), height), cols]

    def whereto(colour, level, step):
        if (colour + level) % 2 == 0:
            return spot(x, (y + step) % 4, z, c)
        return spot((x + step) % 4, y, z, c)

    def position(colour, level):
        return y if (colour + level) % 2 == 0 else x

    def opened(colour, level):
        at = position(colour, level)
        block = block_of(colour, level, at, None)
        base = (colour * 2 + level) * 4
        right = remote(block, block, gring_s.at[base], gring_r.at[base], whereto(colour, level, 1))
        left = remote(block, block, gring_s.at[base + 1], gring_r.at[base + 1], whereto(colour, level, 3))
        right.start()
        left.start()
        return right, left

    def passed(colour, level, pair, tell):
        at = position(colour, level)
        base = (colour * 2 + level) * 4
        right, left = pair
        right.wait_recv()
        block = block_of(colour, level, (at + 3) % 4, 0)
        on_right = remote(block, block, gring_s.at[base + 2], gring_r.at[base + 2], whereto(colour, level, 1))
        on_right.start()
        tell((at + 3) % 4, 1)
        left.wait_recv()
        block = block_of(colour, level, (at + 1) % 4, 1)
        on_left = remote(block, block, gring_s.at[base + 3], gring_r.at[base + 3], whereto(colour, level, 3))
        on_left.start()
        tell((at + 1) % 4, 2)
        return on_right, on_left

    def closed(colour, level, pair, onward, tell):
        at = position(colour, level)
        for copy in onward:
            copy.wait_recv()
        tell((at + 2) % 4, 3)
        for copy in pair + onward:
            copy.wait_send()

    silent = lambda index, slot: None
    low = [opened(colour, 0) for colour in (0, 1)]
    arrive(1, 0)
    low_on = [passed(colour, 0, low[colour], silent) for colour in (0, 1)]
    depart(1, 2)
    for colour in (0, 1):
        closed(colour, 0, low[colour], low_on[colour], silent)
    tails = []

    def teller(colour):
        def tell(index, slot):
            block = block_of(colour, 1, index, None)
            at = colour * 4 + slot
            copy = remote(block, block, tail_s.at[at], tail_r.at[at], partner)
            copy.start()
            tails.append(copy)

        return tell

    high = [opened(colour, 1) for colour in (0, 1)]
    for colour in (0, 1):
        teller(colour)(position(colour, 1), 0)
    depart(1, 3)
    arrive(1, 1)
    high_on = [passed(colour, 1, high[colour], teller(colour)) for colour in (0, 1)]
    forward(1, 0)
    for colour in (0, 1):
        closed(colour, 1, high[colour], high_on[colour], teller(colour))
    arrive(1, 2)
    for copy in tails:
        copy.wait()
    forward(1, 1)
    arrive(1, 3)

    normed = xhat_ref[...].astype(bf)

    def point(n, carry):
        cols = columns_of(n, 256)
        value = jnp.dot(normed, full_ref[:, :, cols].reshape(1024, 256), preferred_element_type=f32)
        gate = jnp.dot(normed, full_ref[:, :, columns_of(n + 4, 256)].reshape(1024, 256), preferred_element_type=f32)
        sig = jax.nn.sigmoid(gate)
        value_ref[:, cols] = value
        sig_ref[:, cols] = sig
        gated_ref[16:144, cols] = value * sig * mask
        return carry

    lax.fori_loop(0, 4, point, 0)
    small = full_ref[:, :, 2048:2176].reshape(1024, 128)
    taps_ref[...] = lax.dot_general(identity(), small, (((1,), (1,)), ((), ())), preferred_element_type=f32)
    forward(1, 2)

    def depth(n, carry):
        cols = columns_of(n, 128)
        total = jnp.zeros((128, 128), f32)
        for k in range(KERNEL):
            total = total + taps_ref[64 + k : 65 + k, cols] * gated_ref[k + 1 : k + 129, cols]
        conv_ref[:, cols] = total
        mixed_ref[:, cols] = (frames_ref[:, cols].astype(f32) + swish_of(total) * mask).astype(bf)
        return carry

    lax.fori_loop(0, 8, depth, 0)
    logits = jnp.dot(mixed_ref[...], small, preferred_element_type=f32)
    scores = [jax.nn.sigmoid(jnp.sum(jnp.where(pick, logits, 0.0), axis=1, keepdims=True)) for pick in picks]
    score_sum = scores[0] + scores[1]
    weights = [score / score_sum for score in scores]
    lane = lax.broadcasted_iota(jnp.int32, shape, 1)
    def fill(n, carry):
        cols = columns_of(n, 256)
        rows_buf[:, cols] = lax.dot_general(both, mixed_ref[:, cols], down, preferred_element_type=f32).astype(bf)
        return carry

    lax.fori_loop(0, 4, fill, 0)
    total = jnp.zeros((256, 128), f32)
    for k in (0, 1):
        upper = weights[k].astype(bf).astype(f32)
        parts = jnp.where(lane == 0, upper, jnp.where(lane == 1, weights[k] - upper, 0.0)).astype(bf)
        total = total + lax.dot_general(spots[k], parts, down, preferred_element_type=f32)
    rows_buf[:, 1024:TALL] = total.astype(bf)
    for q in range(4):
        depart(0, q)
    forward(1, 3)

    folds = {}

    def push(name, q, source, target, where):
        copy = remote(source, target, fold_s.at[name, q], fold_r.at[name, q], where)
        copy.start()
        folds[name, q] = copy

    def compute(q):
        ys = source_y(q)
        for kind in (1, 0):
            for side in (2, 3):
                rings[kind, side, q].wait_recv()

        def scale(n, carry):
            parts = slots[n, ys, :, 1024:TALL].astype(f32)
            weight = parts[:, 0:1] + parts[:, 1:2]
            scaled[n, ys] = (cots[n, ys].astype(f32) * weight).astype(bf)
            return carry

        lax.fori_loop(0, 4, scale, 0)

        def first(n, carry):
            cols = pl.ds(pl.multiple_of(n * 256, 256), 256)
            hidden = jnp.dot(slots[:, ys, :, 0:1024].reshape(256, 1024), inner[:, cols], preferred_element_type=f32)
            act_grad = lax.dot_general(
                scaled[:, ys].reshape(256, 1024), outer[cols, :], (((1,), (1,)), ((), ())), preferred_element_type=f32
            )
            sig = jax.nn.sigmoid(hidden)
            active[:, ys, :, cols] = (hidden * sig).astype(bf).reshape(4, 64, 256)
            slope = sig * (1.0 + hidden * (1.0 - sig))
            pre[:, ys, :, cols] = (act_grad * slope).astype(bf).reshape(4, 64, 256)
            return carry

        lax.fori_loop(0, 4, first, 0)
        def second(n, carry):
            cols = pl.ds(pl.multiple_of(n * 256, 256), 256)
            out = jnp.dot(active[:, ys].reshape(256, 1024), outer[:, cols], preferred_element_type=f32)
            part_y[q, :, :, cols] = out.astype(bf).reshape(4, 64, 256)
            out = lax.dot_general(
                pre[:, ys].reshape(256, 1024), inner[cols, :], (((1,), (1,)), ((), ())), preferred_element_type=f32
            )
            part_z[q, :, :, cols] = out.astype(bf).reshape(4, 64, 256)
            return carry

        lax.fori_loop(0, 4, second, 0)
        push(2, q, part_y.at[q, far], relay_y.at[q], to_right)
        push(3, q, part_z.at[q, far], relay_z.at[q], to_left)
        push(0, q, part_z.at[q, right], straight_z.at[q], to_right)
        push(1, q, part_y.at[q, left], straight_y.at[q], to_left)

    def relay(q):
        folds[2, q].wait_recv()
        part_y[q, right] = (part_y[q, right].astype(f32) + relay_y[q].astype(f32)).astype(bf)
        push(4, q, part_y.at[q, right], joint_y.at[q], to_right)
        folds[3, q].wait_recv()
        part_z[q, left] = (part_z[q, left].astype(f32) + relay_z[q].astype(f32)).astype(bf)
        push(5, q, part_z.at[q, left], joint_z.at[q], to_left)

    def deliver(q):
        yt = source_y(q)
        for name in (1, 4, 0, 5):
            folds[name, q].wait_recv()
        part_y[q, x] = (part_y[q, x].astype(f32) + straight_y[q].astype(f32) + joint_y[q].astype(f32)).astype(bf)
        part_z[q, x] = (part_z[q, x].astype(f32) + straight_z[q].astype(f32) + joint_z[q].astype(f32)).astype(bf)

        def back(i, carry):
            zt, ct = (z + 4 + i // 2) % 8, (c + i) % 2
            rows = pl.ds(pl.multiple_of(8 * zt + 4 * ct, 4), 4)
            for kind, (source, target) in enumerate(((part_y, y_ref), (part_z, z_ref))):
                remote(
                    source.at[q, x, rows], target.at[pl.ds(own4, 4)], back_s.at[kind], back_r.at[kind], (x, yt * 16 + zt * 2 + ct)
                ).start()
            return carry

        if STEPS[q] == 0:
            lax.fori_loop(0, 8, back, 0)
            lax.fori_loop(9, 16, back, 0)
            for kind, (source, target) in enumerate(((part_y, y_ref), (part_z, z_ref))):
                copy = pltpu.make_async_copy(
                    source.at[q, x, pl.ds(line4, 4)], target.at[pl.ds(own4, 4)], self_s.at[2 + kind]
                )
                copy.start()
                selfs[2 + kind] = copy
        else:
            lax.fori_loop(0, 16, back, 0)

    stores = []

    def weight_grad(which, left_ref, right_ref, target):
        def body(n, carry):
            cols = pl.ds(pl.multiple_of(n * 256, 256), 256)
            out = lax.dot_general(
                left_ref[:, :, :, cols].reshape(1024, 256),
                right_ref[...].reshape(1024, 1024),
                (((0,), (0,)), ((), ())),
                preferred_element_type=f32,
            )
            grad_buf[which, cols, :] = out.astype(bf)
            return carry

        lax.fori_loop(0, 4, body, 0)
        copy = pltpu.make_async_copy(grad_buf.at[which], target, store_sem.at[which])
        copy.start()
        stores.append(copy)

    for load in loads:
        load.wait()
    arrive(0, 0)
    arrive(0, 1)
    forward(0, 0)
    arrive(0, 2)
    forward(0, 1)
    compute(0)
    arrive(0, 3)
    forward(0, 2)
    compute(1)
    relay(0)
    forward(0, 3)
    compute(2)
    relay(1)
    deliver(0)
    compute(3)
    relay(2)
    turned[...] = jnp.transpose(xhat_ref[...]).astype(bf)
    deliver(1)
    weight_grad(1, active, scaled, outer_grad_hbm)
    relay(3)
    deliver(2)
    weight_grad(0, slots, pre, inner_grad_hbm)
    deliver(3)
    for kind in (0, 1):
        view = sized.at[pl.ds(0, 63), :, pl.ds(0, 1024)]
        remote(view, view, back_s.at[kind], back_r.at[kind], to_right).wait()
    for copy in (selfs[2], selfs[3]):
        copy.wait()

    def output(n, carry):
        cols = columns_of(n, 256)
        og = og_ref[:, cols].astype(f32)
        total = jnp.zeros((128, 256), f32)
        sums = []
        for k in (0, 1):
            picked = jnp.dot(spots[k], y_ref[:, cols], preferred_element_type=f32)
            total = total + weights[k] * picked
            sums.append(carry[k] + jnp.sum(og * picked, axis=1, keepdims=True))
        layer_ref[:, cols] = (mixed_ref[:, cols].astype(f32) + total).astype(bf)
        return tuple(sums)

    start = jnp.zeros((128, 1), f32)
    weight_sums = lax.fori_loop(0, 4, output, (start, start))
    mean_term = weight_sums[0] * weights[0] + weight_sums[1] * weights[1]
    logit_grad = jnp.zeros((128, 128), f32)
    for k in (0, 1):
        chosen = (weight_sums[k] - mean_term) / score_sum * scores[k] * (1.0 - scores[k])
        logit_grad = jnp.where(picks[k], chosen, logit_grad)
    logit_grad = logit_grad.astype(bf)
    across = (((1,), (1,)), ((), ()))

    def mix(n, carry):
        cols = columns_of(n, 256)
        grad = og_ref[:, cols].astype(f32) + jnp.dot(both, z_ref[:, cols], preferred_element_type=f32)
        grad = grad + lax.dot_general(logit_grad, full_ref[n, :, 2048:2176], across, preferred_element_type=f32)
        mg_buf[:, cols] = grad
        cg_buf[16:144, cols] = grad * mask * swish_slope(conv_ref[:, cols])
        return carry

    lax.fori_loop(0, 4, mix, 0)

    def depth_back(n, carry):
        cols = columns_of(n, 128)
        grad = cg_buf[16:144, cols]
        total = jnp.zeros((128, 128), f32)
        for k in range(KERNEL):
            total = total + taps_ref[64 + k : 65 + k, cols] * cg_buf[31 - k : 159 - k, cols]
            tg_buf[64 + k : 65 + k, cols] = jnp.sum(grad * gated_ref[k + 1 : k + 129, cols], axis=0, keepdims=True)
        total = total * mask
        sig = sig_ref[:, cols]
        pc_buf[:, cols] = (total * sig).astype(bf)
        pc_buf[:, columns_of(n + 8, 128)] = (total * value_ref[:, cols] * sig * (1.0 - sig)).astype(bf)
        return carry

    lax.fori_loop(0, 8, depth_back, 0)
    out = lax.dot_general(mixed_ref[...], logit_grad, down, preferred_element_type=f32)
    out = out + lax.dot_general(tg_buf[...].astype(bf), identity(), down, preferred_element_type=f32)
    part_ref[:, :, 2048:2176] = out.astype(bf).reshape(4, 256, 128)

    def outer_product(i, carry):
        cols = columns_of((i + 9 * (1 - c)) % 16, 128)
        out = jnp.dot(turned[...], pc_buf[:, cols], preferred_element_type=f32)
        part_ref[:, :, cols] = out.astype(bf).reshape(4, 256, 128)
        return carry

    lax.fori_loop(0, 9, outer_product, 0)
    colours = ((0, SPLIT), (SPLIT, HALF - SPLIT))
    order = (2, 1, 3, 0)

    def rows_of(colour, index):
        if colour == 0:
            return index, pl.ds(0, 256)
        return slice(None), pl.ds(pl.multiple_of(index * 64, 64), 64)

    swaps = {}
    for step in order:
        for colour, (begin, width) in enumerate(colours):
            at = ((x if colour == 0 else y) + step) % 4
            lead, rows = rows_of(colour, at)
            slot = colour * 4 + step
            copy = remote(
                part_ref.at[lead, rows, pl.ds(pl.multiple_of(other + begin, 128), width)],
                swap_buf.at[lead, rows, pl.ds(begin, width)],
                swap_s.at[slot],
                swap_r.at[slot],
                partner,
            )
            copy.start()
            swaps[colour, step] = copy

    lax.fori_loop(9, 16, outer_product, 0)

    def inward(n, carry):
        cols = columns_of(n, 256)
        out = lax.dot_general(pc_buf[...], full_ref[n, :, 0:2048], across, preferred_element_type=f32)
        ng_buf[:, cols] = out
        first = carry[0] + jnp.sum(out, axis=1, keepdims=True)
        second = carry[1] + jnp.sum(out * xhat_ref[:, cols], axis=1, keepdims=True)
        return first, second

    def finish_frames():
        first, second = lax.fori_loop(0, 4, inward, (start, start))
        first, second = first * (1.0 / 1024), second * (1.0 / 1024)

        def finish(n, carry):
            cols = columns_of(n, 256)
            grad = inv_scale * (ng_buf[:, cols] - first - xhat_ref[:, cols] * second)
            frames_grad_ref[:, cols] = (mg_buf[:, cols] + grad).astype(bf)
            return carry

        lax.fori_loop(0, 4, finish, 0)

    def first_to(colour, step):
        if colour == 0:
            return spot((x + step) % 4, y, z, c)
        return spot(x, (y + step) % 4, z, c)

    def second_to(colour, step):
        return first_to(1 - colour, step)

    def fold(colour, step, extra):
        begin, width = colours[colour]
        at = ((x if colour == 0 else y) + step) % 4
        swaps[colour, step].wait_recv()

        def body(t, carry):
            if colour == 0:
                lead, row = at, pl.multiple_of(t * 32, 32)
            else:
                lead, row = t // 2, pl.multiple_of(at * 64 + (t % 2) * 32, 32)
            value = part_ref[lead, pl.ds(row, 32), pl.ds(pl.multiple_of(mine + begin, 128), width)].astype(jnp.float32)
            value = value + swap_buf[lead, pl.ds(row, 32), pl.ds(begin, width)].astype(jnp.float32)
            value = extra(t, value)
            half_buf[colour, step, pl.ds(pl.multiple_of(t * 32, 32), 32), pl.ds(0, width)] = value.astype(jnp.bfloat16)
            return carry

        return body

    plain = lambda t, value: value
    sent = []
    pend = {}
    for colour, (begin, width) in enumerate(colours):
        lax.fori_loop(0, 8, fold(colour, 2, plain), 0)
        for side, step in ((0, 1), (1, 3)):
            slot = colour * 8 + side
            copy = remote(
                half_buf.at[colour, 2, pl.ds(side * 128, 128), pl.ds(0, width)],
                far_buf.at[colour, side, :, pl.ds(0, width)],
                rring_s.at[slot],
                rring_r.at[slot],
                first_to(colour, step),
            )
            copy.start()
            pend[colour, side] = copy
            sent.append(copy)
    finish_frames()
    for colour, (begin, width) in enumerate(colours):
        for side, step in ((0, 1), (1, 3)):
            lo = side * 4

            lax.fori_loop(4 - lo, 8 - lo, fold(colour, step, plain), 0)
            pend[colour, side].wait_recv()

            def extra(t, value, colour=colour, side=side, lo=lo, width=width):
                row = pl.multiple_of((t - lo) * 32, 32)
                return value + far_buf[colour, side, pl.ds(row, 32), pl.ds(0, width)].astype(jnp.float32)

            def again(t, carry, colour=colour, step=step, extra=extra, begin=begin, width=width):
                at = ((x if colour == 0 else y) + step) % 4
                if colour == 0:
                    lead, row = at, pl.multiple_of(t * 32, 32)
                else:
                    lead, row = t // 2, pl.multiple_of(at * 64 + (t % 2) * 32, 32)
                value = part_ref[lead, pl.ds(row, 32), pl.ds(pl.multiple_of(mine + begin, 128), width)].astype(jnp.float32)
                value = value + swap_buf[lead, pl.ds(row, 32), pl.ds(begin, width)].astype(jnp.float32)
                value = extra(t, value)
                half_buf[colour, step, pl.ds(pl.multiple_of(t * 32, 32), 32), pl.ds(0, width)] = value.astype(jnp.bfloat16)
                return carry

            lax.fori_loop(lo, lo + 4, again, 0)
            slot = colour * 8 + 2 + side
            copy = remote(
                half_buf.at[colour, step, :, pl.ds(0, width)],
                near_buf.at[colour, side, :, pl.ds(0, width)],
                rring_s.at[slot],
                rring_r.at[slot],
                first_to(colour, step),
            )
            copy.start()
            pend[colour, 2 + side] = copy
            sent.append(copy)
    for colour, (begin, width) in enumerate(colours):
        pend[colour, 2].wait_recv()
        pend[colour, 3].wait_recv()

        def extra(t, value, colour=colour, width=width):
            row = pl.multiple_of(t * 32, 32)
            for side in (0, 1):
                value = value + near_buf[colour, side, pl.ds(row, 32), pl.ds(0, width)].astype(jnp.float32)
            return value

        body = fold(colour, 0, extra)
        lax.fori_loop(0, 8, body, 0)
        at = y if colour == 0 else x
        for side, step in ((0, 1), (1, 3)):
            row = pl.multiple_of(((at + 2) % 4) * 64 + side * 32, 32)
            slot = colour * 8 + 4 + side
            copy = remote(
                half_buf.at[colour, 0, pl.ds(row, 32), pl.ds(0, width)],
                mid_far.at[colour, side, :, pl.ds(0, width)],
                rring_s.at[slot],
                rring_r.at[slot],
                second_to(colour, step),
            )
            copy.start()
            pend[colour, 4 + side] = copy
            sent.append(copy)
    for colour, (begin, width) in enumerate(colours):
        at = y if colour == 0 else x
        for side, step in ((0, 1), (1, 3)):
            row = pl.multiple_of(((at + step) % 4) * 64, 32)
            pend[colour, 4 + side].wait_recv()
            for piece in (0, 1):
                value = half_buf[colour, 0, pl.ds(pl.multiple_of(row + piece * 32, 32), 32), pl.ds(0, width)]
                if piece == side:
                    value = value.astype(jnp.float32) + mid_far[colour, side, :, pl.ds(0, width)].astype(jnp.float32)
                    value = value.astype(jnp.bfloat16)
                mid_buf[colour, side, pl.ds(piece * 32, 32), pl.ds(0, width)] = value
            slot = colour * 8 + 6 + side
            copy = remote(
                mid_buf.at[colour, side, :, pl.ds(0, width)],
                mid_near.at[colour, side, :, pl.ds(0, width)],
                rring_s.at[slot],
                rring_r.at[slot],
                second_to(colour, step),
            )
            copy.start()
            pend[colour, 6 + side] = copy
            sent.append(copy)
    for colour, (begin, width) in enumerate(colours):
        at = y if colour == 0 else x
        pend[colour, 6].wait_recv()
        pend[colour, 7].wait_recv()
        for piece in range(2):
            rows = pl.ds(piece * 32, 32)
            value = half_buf[colour, 0, pl.ds(pl.multiple_of(at * 64 + piece * 32, 32), 32), pl.ds(0, width)].astype(jnp.float32)
            for side in (0, 1):
                value = value + mid_near[colour, side, rows, pl.ds(0, width)].astype(jnp.float32)
            z_src[pl.ds(piece * 4, 4), :, pl.ds(begin, width)] = value.astype(jnp.bfloat16).reshape(4, 8, width)
    z_copies = []
    for dz in (4, 3, 5, 2, 6, 1, 7):
        to = (z + dz) % 8
        copy = remote(z_src.at[to], z_buf.at[dz - 1], rz_s.at[dz - 1], rz_r.at[dz - 1], spot(x, y, to, c))
        copy.start()
        z_copies.append(copy)
    total = z_src[z].astype(jnp.float32)
    for copy in z_copies:
        copy.wait_recv()
    for k in range(7):
        total = total + z_buf[k].astype(jnp.float32)
    last_src[...] = total
    last = remote(last_src, last_buf, last_s, last_r, partner)
    last.start()
    for copy in sent + z_copies:
        copy.wait_send()
    for copy in swaps.values():
        copy.wait_send()
    kept = jnp.where(c == 0, last_src[0:4, :], last_src[4:8, :])
    last.wait()
    got = jnp.where(c == 0, last_buf[0:4, :], last_buf[4:8, :])
    low, high = jnp.where(c == 0, kept, got), jnp.where(c == 0, got, kept)
    out_ref[:, 0:HALF] = low
    out_ref[:, HALF:2048] = high[:, 0 : 2048 - HALF]
    router_grad_ref[...] = high[:, 2048 - HALF : 2112 - HALF]
    depth_ref[...] = high[:, 2112 - HALF : 2112 + KERNEL - HALF]
    for kind in (0, 1):
        for q in range(4):
            view = bulk(kind, q)
            remote(view, view, there_s.at[kind, q], there_r.at[kind, q], to_right).wait_send()
    for copy in list(rings.values()) + list(folds.values()):
        copy.wait_send()
    for copy in stores:
        copy.wait()


def layer(frames, lengths, ids, og, conv_in, router, depthwise, inner, outer):
    dma, bf, f32 = pltpu.SemaphoreType.DMA, jnp.bfloat16, jnp.float32
    block = lambda *lead: pltpu.VMEM(lead + (64, 1024), bf)
    shape = lambda *args: jax.ShapeDtypeStruct(*args)
    vmem, anywhere = pl.BlockSpec(memory_space=pltpu.VMEM), pl.BlockSpec(memory_space=pl.ANY)
    wide = pltpu.VMEM((128, 1024), f32)
    long = pltpu.VMEM((160, 1024), f32)
    half = lambda *lead: pltpu.VMEM(lead + (SPLIT,), bf)
    return pl.pallas_call(
        layer_kernel,
        out_shape=(
            shape((128, 1024), bf), shape((128, 1024), bf), shape((4, 2048), f32), shape((4, KERNEL), f32),
            shape((4, 64), f32), shape((1024, 1024), bf), shape((1024, 1024), bf),
        ),
        in_specs=[vmem, pl.BlockSpec(memory_space=pltpu.SMEM)] + [vmem] * 5 + [anywhere] * 2,
        out_specs=(vmem,) * 5 + (anywhere,) * 2,
        scratch_shapes=[
            pltpu.VMEM((4, 256, WIDE), bf), pltpu.VMEM((128, 1024), bf), wide, wide, wide, wide, long, wide,
            pltpu.VMEM((256, 1024), bf), pltpu.VMEM((256, 1024), bf),
            pltpu.VMEM((4, WIDE), bf), pltpu.VMEM((256, TALL), bf), pltpu.VMEM((256, 1024), bf),
            pltpu.VMEM((4, 4, 64, TALL), bf),
        ]
        + [block(4, 4)] * 4
        + [pltpu.VMEM((1024, 1024), bf)] * 2
        + [block(4, 4)] * 2
        + [block(4)] * 6
        + [pltpu.VMEM((2, 1024, 1024), bf), pltpu.VMEM((63, 4, TALL), bf)]
        + [wide, long, wide, pltpu.VMEM((128, 2048), bf), pltpu.VMEM((1024, 128), bf), wide]
        + [
            pltpu.VMEM((4, 256, WIDE), bf), pltpu.VMEM((4, 256, HALF), bf), half(2, 4, 256), half(2, 2, 128),
            half(2, 2, 256), half(2, 2, 64), half(2, 2, 32), half(2, 2, 64), pltpu.VMEM((8, 8, HALF), bf),
            pltpu.VMEM((7, 8, HALF), bf), pltpu.VMEM((8, HALF), f32), pltpu.VMEM((8, HALF), f32),
        ]
        + [
            dma((2,)), dma, dma, dma, dma((7,)), dma((7,)), dma((16,)), dma((16,)), dma((8,)), dma((8,)),
            dma((4,)), dma((2, 4)), dma((2, 4)), dma((2, 4, 4)), dma((2, 4, 4)), dma((6, 4)), dma((6, 4)), dma((2,)),
            dma((2,)), dma((2,)), dma((8,)), dma((8,)), dma((16,)), dma((16,)), dma((7,)), dma((7,)), dma, dma,
        ],
        compiler_params=pltpu.CompilerParams(
            collective_id=2, has_side_effects=True, vmem_limit_bytes=VMEM_LIMIT
        ),
        name="layer",
    )(frames, lengths, ids, og, conv_in, router, depthwise, inner, outer)


def pass_kernel(*refs):
    sources, targets, bufs, sems = refs[:7], refs[7:14], refs[14:21], refs[21]
    loads, stores = [], []
    for i in range(7):
        for part in range(4 if i >= 5 else 1):
            pick = (lambda ref: ref) if i < 5 else (lambda ref: ref.at[pl.ds(part * 256, 256)])
            at = len(loads)
            loads.append(pltpu.make_async_copy(pick(sources[i]), pick(bufs[i]), sems.at[0, at]))
            stores.append(pltpu.make_async_copy(pick(bufs[i]), pick(targets[i]), sems.at[1, at]))
    order = list(range(5, 13)) + list(range(5))
    for at in order:
        loads[at].start()
    for at in order:
        loads[at].wait()
        stores[at].start()
    for at in order:
        stores[at].wait()


def pass_on(values):
    shapes = tuple(jax.ShapeDtypeStruct(value.shape, value.dtype) for value in values)
    anywhere = pl.BlockSpec(memory_space=pl.ANY)
    return pl.pallas_call(
        pass_kernel,
        out_shape=shapes,
        in_specs=[anywhere] * 7,
        out_specs=(anywhere,) * 7,
        scratch_shapes=[pltpu.VMEM(value.shape, value.dtype) for value in values] + [pltpu.SemaphoreType.DMA((2, 13))],
        compiler_params=pltpu.CompilerParams(vmem_limit_bytes=VMEM_LIMIT),
        name="pass_on",
    )(*values)


def per_device(frames, lengths, expert_ids, conv_in, depthwise, router, w_in, w_out, out_grad):
    *outs, w_in_grad, w_out_grad = pass_on(
        layer(frames, lengths, expert_ids, out_grad, conv_in, router, depthwise, w_in[0], w_out[0])
    )
    return (*outs, w_in_grad[None], w_out_grad[None])


def solution(mesh):
    in_specs = (
        P(("dp", "expert"), None),
        P(("dp", "expert")),
        P(("dp", "expert"), None),
        P(("dp", "expert"), None),
        P(("dp", "expert"), None),
        P(("dp", "expert"), None),
        P("expert", None, "dp"),
        P("expert", "dp", None),
        P(("dp", "expert"), None),
    )
    out_specs = (
        P(("dp", "expert"), None),
        P(("dp", "expert"), None),
        P(("dp", "expert"), None),
        P(("dp", "expert"), None),
        P(("dp", "expert"), None),
        P("expert", None, "dp"),
        P("expert", "dp", None),
    )
    return jax.shard_map(
        per_device, mesh=mesh, in_specs=in_specs, out_specs=out_specs, check_vma=False
    )
```

time: 203 us -> 185 us (0.911)
  Pallas kernels: 196 us -> 183 us
  local copies, waits for them, and re-layouts: 5.26 us -> 1.41 us
    pallas_call x3 -> x2, Pallas kernels: 196 us -> 183 us  [the longest x1 178 us: layer(): pl.pallas_call(layer_kernel, out_shape=(shape((128, 1024), bf), shape((12...]
    unnamed x4 -> x1, local copies, waits for them, and re-layouts: 5.26 us -> 1.41 us
where the time goes in v3:
time: 185 us
  Pallas kernels  183 us (99%)
    pallas_call x1, Pallas kernels, layer(): pl.pallas_call(layer_kernel, out_shape=(shape((128, 1024), bf), shape((12...  178 us
    pallas_call x1, Pallas kernels, pass_on(): pl.pallas_call(pass_kernel, out_shape=shapes, in_specs=[anywhere] * 7, ou...  4.13 us

profile of v3, /device:TPU:1, one launch (start us, length us, event | category | flops | bytes accessed | tf_op | source)
XLA Modules:
  0.0 185.3 jit_solution(8675331910039992826)
XLA Ops:
  1.3 1.4 copy.16.ids_ref
  2.7 178.4 %layer.1 = (bf16[128,1024]{1,0:T(8,128)(2,1)}, bf16[128,1024]{1,0:T(8,128)(2,1)}, f32[4,2048]{1,0:T(4,128)}, f32[4,31]{1,0:T(4,128)}, f32[4,64]{1,0:T(4,128)}, /...) custom-call(bf16[128,1024]{1,0:T(8,128)(2,1)} %frames_ref.1, s32[1]{0:T(128)S(6)} %copy.17.length_ref, ...), custom_call_target="tpu_custom_call" | custom-call | tf_op jit(solution)/shard_map/layer/pallas_call | solution.py:791
  181.1 4.1 %pass_on.1 = (bf16[128,1024]{1,0:T(8,128)(2,1)}, bf16[128,1024]{1,0:T(8,128)(2,1)}, f32[4,2048]{1,0:T(4,128)}, f32[4,31]{1,0:T(4,128)}, f32[4,64]{1,0:T(4,128)},...) custom-call(bf16[128,1024]{1,0:T(8,128)(2,1)} %get-tuple-element.21.refs_0_, ...), custom_call_target="tpu_custom_call" | custom-call | tf_op jit(solution)/shard_map/pass_on/pallas_call | solution.py:850

commit v4 on v3

--- a/solution.py
+++ b/solution.py
@@ -59,9 +59,11 @@
     return (lax.broadcasted_iota(jnp.int32, (128, 1), 0) < length_ref[0]).astype(jnp.float32)
 
 
-def chosen_of(ids_ref):
-    lane = lax.broadcasted_iota(jnp.int32, (128, 128), 1)
-    return [lane == ids_ref[:, k : k + 1] for k in (0, 1)]
+def index_columns(ids_ref):
+    shape = (128, 128)
+    diagonal = lax.broadcasted_iota(jnp.int32, shape, 0) == lax.broadcasted_iota(jnp.int32, shape, 1)
+    rows = ids_ref[...].astype(jnp.float32)
+    return [jnp.sum(jnp.where(diagonal, rows[k : k + 1, :], 0.0), axis=1, keepdims=True) for k in (0, 1)]
 
 
 def identity():
@@ -106,7 +108,9 @@
         [router_ref[...].astype(f32), depthwise_ref[...].astype(f32), jnp.zeros((4, WIDE - 2112 - KERNEL), f32)], axis=1
     ).astype(bf)
     mask = mask_of(length_ref)
-    picks = chosen_of(ids_ref)
+    index = index_columns(ids_ref)
+    lanes = lax.broadcasted_iota(jnp.int32, (128, 128), 1).astype(f32)
+    picks = [lanes == column for column in index]
     count = (jnp.where(picks[0] | picks[1], 1.0, 0.0) * mask).astype(bf)
     shape = (128, 128)
     below = (lax.broadcasted_iota(jnp.int32, shape, 1) < lax.broadcasted_iota(jnp.int32, shape, 0)).astype(bf)
@@ -116,7 +120,7 @@
     for k, pick in enumerate(picks):
         position = jnp.sum(jnp.where(pick, before, 0.0), axis=1, keepdims=True)
         kept = (position < 4.0) & (mask > 0.0)
-        slot = jnp.where(kept, ids_ref[:, k : k + 1].astype(f32) * 4.0 + position, -1.0)
+        slot = jnp.where(kept, index[k] * 4.0 + position, -1.0)
         slot_of.append(slot)
         spots.append((wide == slot).astype(bf))
     both = spots[0] + spots[1]
@@ -498,11 +502,12 @@
     deliver(2)
     weight_grad(0, slots, pre, inner_grad_hbm)
     deliver(3)
-    for kind in (0, 1):
+    def returned(kind):
         view = sized.at[pl.ds(0, 63), :, pl.ds(0, 1024)]
         remote(view, view, back_s.at[kind], back_r.at[kind], to_right).wait()
-    for copy in (selfs[2], selfs[3]):
-        copy.wait()
+        selfs[2 + kind].wait()
+
+    returned(0)
 
     def output(n, carry):
         cols = columns_of(n, 256)
@@ -534,6 +539,7 @@
         cg_buf[16:144, cols] = grad * mask * swish_slope(conv_ref[:, cols])
         return carry
 
+    returned(1)
     lax.fori_loop(0, 4, mix, 0)
 
     def depth_back(n, carry):
@@ -639,7 +645,7 @@
     for colour, (begin, width) in enumerate(colours):
         lax.fori_loop(0, 8, fold(colour, 2, plain), 0)
         for side, step in ((0, 1), (1, 3)):
-            slot = colour * 8 + side
+            slot = colour * 12 + side
             copy = remote(
                 half_buf.at[colour, 2, pl.ds(side * 128, 128), pl.ds(0, width)],
                 far_buf.at[colour, side, :, pl.ds(0, width)],
@@ -650,12 +656,25 @@
             copy.start()
             pend[colour, side] = copy
             sent.append(copy)
+    for colour, (begin, width) in enumerate(colours):
+        for side, step in ((0, 1), (1, 3)):
+            lax.fori_loop(4 - 4 * side, 8 - 4 * side, fold(colour, step, plain), 0)
+            slot = colour * 12 + 8 + side
+            rows = pl.ds(128 - 128 * side, 128)
+            copy = remote(
+                half_buf.at[colour, step, rows, pl.ds(0, width)],
+                near_buf.at[colour, side, rows, pl.ds(0, width)],
+                rring_s.at[slot],
+                rring_r.at[slot],
+                first_to(colour, step),
+            )
+            copy.start()
+            pend[colour, 8 + side] = copy
+            sent.append(copy)
     finish_frames()
     for colour, (begin, width) in enumerate(colours):
         for side, step in ((0, 1), (1, 3)):
             lo = side * 4
-
-            lax.fori_loop(4 - lo, 8 - lo, fold(colour, step, plain), 0)
             pend[colour, side].wait_recv()
 
             def extra(t, value, colour=colour, side=side, lo=lo, width=width):
@@ -675,10 +694,10 @@
                 return carry
 
             lax.fori_loop(lo, lo + 4, again, 0)
-            slot = colour * 8 + 2 + side
+            slot = colour * 12 + 2 + side
             copy = remote(
-                half_buf.at[colour, step, :, pl.ds(0, width)],
-                near_buf.at[colour, side, :, pl.ds(0, width)],
+                half_buf.at[colour, step, pl.ds(128 * side, 128), pl.ds(0, width)],
+                near_buf.at[colour, side, pl.ds(128 * side, 128), pl.ds(0, width)],
                 rring_s.at[slot],
                 rring_r.at[slot],
                 first_to(colour, step),
@@ -687,8 +706,8 @@
             pend[colour, 2 + side] = copy
             sent.append(copy)
     for colour, (begin, width) in enumerate(colours):
-        pend[colour, 2].wait_recv()
-        pend[colour, 3].wait_recv()
+        for name in (8, 9, 2, 3):
+            pend[colour, name].wait_recv()
 
         def extra(t, value, colour=colour, width=width):
             row = pl.multiple_of(t * 32, 32)
@@ -701,7 +720,7 @@
         at = y if colour == 0 else x
         for side, step in ((0, 1), (1, 3)):
             row = pl.multiple_of(((at + 2) % 4) * 64 + side * 32, 32)
-            slot = colour * 8 + 4 + side
+            slot = colour * 12 + 4 + side
             copy = remote(
                 half_buf.at[colour, 0, pl.ds(row, 32), pl.ds(0, width)],
                 mid_far.at[colour, side, :, pl.ds(0, width)],
@@ -712,21 +731,31 @@
             copy.start()
             pend[colour, 4 + side] = copy
             sent.append(copy)
+        for side, step in ((0, 1), (1, 3)):
+            row = pl.multiple_of(((at + step) % 4) * 64 + 32 - 32 * side, 32)
+            slot = colour * 12 + 10 + side
+            copy = remote(
+                half_buf.at[colour, 0, pl.ds(row, 32), pl.ds(0, width)],
+                mid_near.at[colour, side, pl.ds(32 - 32 * side, 32), pl.ds(0, width)],
+                rring_s.at[slot],
+                rring_r.at[slot],
+                second_to(colour, step),
+            )
+            copy.start()
+            pend[colour, 10 + side] = copy
+            sent.append(copy)
     for colour, (begin, width) in enumerate(colours):
         at = y if colour == 0 else x
         for side, step in ((0, 1), (1, 3)):
-            row = pl.multiple_of(((at + step) % 4) * 64, 32)
+            row = pl.multiple_of(((at + step) % 4) * 64 + 32 * side, 32)
             pend[colour, 4 + side].wait_recv()
-            for piece in (0, 1):
-                value = half_buf[colour, 0, pl.ds(pl.multiple_of(row + piece * 32, 32), 32), pl.ds(0, width)]
-                if piece == side:
-                    value = value.astype(jnp.float32) + mid_far[colour, side, :, pl.ds(0, width)].astype(jnp.float32)
-                    value = value.astype(jnp.bfloat16)
-                mid_buf[colour, side, pl.ds(piece * 32, 32), pl.ds(0, width)] = value
-            slot = colour * 8 + 6 + side
+            value = half_buf[colour, 0, pl.ds(row, 32), pl.ds(0, width)].astype(f32)
+            value = value + mid_far[colour, side, :, pl.ds(0, width)].astype(f32)
+            mid_buf[colour, side, pl.ds(32 * side, 32), pl.ds(0, width)] = value.astype(bf)
+            slot = colour * 12 + 6 + side
             copy = remote(
-                mid_buf.at[colour, side, :, pl.ds(0, width)],
-                mid_near.at[colour, side, :, pl.ds(0, width)],
+                mid_buf.at[colour, side, pl.ds(32 * side, 32), pl.ds(0, width)],
+                mid_near.at[colour, side, pl.ds(32 * side, 32), pl.ds(0, width)],
                 rring_s.at[slot],
                 rring_r.at[slot],
                 second_to(colour, step),
@@ -736,8 +765,8 @@
             sent.append(copy)
     for colour, (begin, width) in enumerate(colours):
         at = y if colour == 0 else x
-        pend[colour, 6].wait_recv()
-        pend[colour, 7].wait_recv()
+        for name in (10, 11, 6, 7):
+            pend[colour, name].wait_recv()
         for piece in range(2):
             rows = pl.ds(piece * 32, 32)
             value = half_buf[colour, 0, pl.ds(pl.multiple_of(at * 64 + piece * 32, 32), 32), pl.ds(0, width)].astype(jnp.float32)
@@ -816,7 +845,7 @@
         + [
             dma((2,)), dma, dma, dma, dma((7,)), dma((7,)), dma((16,)), dma((16,)), dma((8,)), dma((8,)),
             dma((4,)), dma((2, 4)), dma((2, 4)), dma((2, 4, 4)), dma((2, 4, 4)), dma((6, 4)), dma((6, 4)), dma((2,)),
-            dma((2,)), dma((2,)), dma((8,)), dma((8,)), dma((16,)), dma((16,)), dma((7,)), dma((7,)), dma, dma,
+            dma((2,)), dma((2,)), dma((8,)), dma((8,)), dma((24,)), dma((24,)), dma((7,)), dma((7,)), dma, dma,
         ],
         compiler_params=pltpu.CompilerParams(
             collective_id=2, has_side_effects=True, vmem_limit_bytes=VMEM_LIMIT
@@ -860,7 +889,7 @@
 
 def per_device(frames, lengths, expert_ids, conv_in, depthwise, router, w_in, w_out, out_grad):
     *outs, w_in_grad, w_out_grad = pass_on(
-        layer(frames, lengths, expert_ids, out_grad, conv_in, router, depthwise, w_in[0], w_out[0])
+        layer(frames, lengths, expert_ids.T, out_grad, conv_in, router, depthwise, w_in[0], w_out[0])
     )
     return (*outs, w_in_grad[None], w_out_grad[None])
 

time: 185 us -> 181 us (0.978)
  Pallas kernels: 183 us -> 180 us
    pallas_call x1, Pallas kernels: 178 us -> 175 us  [layer(): pl.pallas_call(layer_kernel, out_shape=(shape((128, 1024), bf), shape((12...]
where the time goes in v4:
time: 181 us
  Pallas kernels  180 us (99%)
    pallas_call x1, Pallas kernels, layer(): pl.pallas_call(layer_kernel, out_shape=(shape((128, 1024), bf), shape((12...  175 us
    pallas_call x1, Pallas kernels, pass_on(): pl.pallas_call(pass_kernel, out_shape=shapes, in_specs=[anywhere] * 7, ou...  4.13 us

profile of v4, /device:TPU:1, one launch (start us, length us, event | category | flops | bytes accessed | tf_op | source)
XLA Modules:
  0.0 180.9 jit_solution(8994399410869472314)
XLA Ops:
  1.3 175.4 %layer.1 = (bf16[128,1024]{1,0:T(8,128)(2,1)}, bf16[128,1024]{1,0:T(8,128)(2,1)}, f32[4,2048]{1,0:T(4,128)}, f32[4,31]{1,0:T(4,128)}, f32[4,64]{1,0:T(4,128)}, /...) custom-call(bf16[128,1024]{1,0:T(8,128)(2,1)} %frames_ref.1, s32[1]{0:T(128)S(6)} %copy.16.length_ref, ...), custom_call_target="tpu_custom_call" | custom-call | tf_op jit(solution)/shard_map/layer/pallas_call | solution.py:820
  176.7 4.1 %pass_on.1 = (bf16[128,1024]{1,0:T(8,128)(2,1)}, bf16[128,1024]{1,0:T(8,128)(2,1)}, f32[4,2048]{1,0:T(4,128)}, f32[4,31]{1,0:T(4,128)}, f32[4,64]{1,0:T(4,128)},...) custom-call(bf16[128,1024]{1,0:T(8,128)(2,1)} %get-tuple-element.21.refs_0_, ...), custom_call_target="tpu_custom_call" | custom-call | tf_op jit(solution)/shard_map/pass_on/pallas_call | solution.py:879

commit v5 on v4

--- a/solution.py
+++ b/solution.py
@@ -77,9 +77,9 @@
     full_ref, mixed_ref, value_ref, sig_ref, conv_ref, xhat_ref, gated_ref, taps_ref, y_ref, z_ref,
     own_ref, rows_buf, og_rows, slots, cots, scaled, active, pre, inner, outer, part_y, part_z, straight_y, straight_z,
     relay_y, relay_z, joint_y, joint_z, grad_buf, sized, mg_buf, cg_buf, tg_buf, pc_buf, turned, ng_buf,
-    part_ref, swap_buf, half_buf, far_buf, near_buf, mid_buf, mid_far, mid_near, z_src, z_buf, last_src, last_buf,
-    load_sem, core_s, core_r, own_sem, z_s, z_r, gring_s, gring_r, tail_s, tail_r, self_s, there_s, there_r, ring_s,
-    ring_r, fold_s, fold_r, back_s, back_r, store_sem, swap_s, swap_r, rring_s, rring_r, rz_s, rz_r, last_s, last_r
+    part_ref, swap_buf, half_buf, far_buf, near_buf, mid_buf, mid_far, mid_near, z_src, z_buf,
+    slope_buf, load_sem, own_sem, z_s, z_r, gring_s, gring_r, tail_s, tail_r, self_s, there_s, there_r, ring_s,
+    ring_r, fold_s, fold_r, back_s, back_r, store_sem, swap_s, swap_r, rring_s, rring_r, rz_s, rz_r
 ):
     x, y, z, c = place()
     f32, bf = jnp.float32, jnp.bfloat16
@@ -194,27 +194,26 @@
     other = pl.multiple_of((1 - c) * HALF, 128)
     row = pl.multiple_of(y * 64 + z * 8, 8)
     row4 = pl.multiple_of(row + 4 * c, 4)
-    swap = remote(
-        own_ref.at[:, pl.ds(other, HALF)],
-        full_ref.at[x, pl.ds(row4, 4), pl.ds(other, HALF)],
-        core_s,
-        core_r,
-        partner,
-    )
-    swap.start()
     keep = pltpu.make_async_copy(
         own_ref.at[:, pl.ds(mine, HALF)], full_ref.at[x, pl.ds(row4, 4), pl.ds(mine, HALF)], own_sem
     )
     keep.start()
+    copies = []
+    for dz in (4, 3, 5, 2, 6, 1, 7, 0):
+        for dc, begin in ((0, mine), (1, other)):
+            if dz or dc:
+                at = 2 * dz + dc
+                copy = remote(
+                    own_ref.at[:, pl.ds(begin, HALF)],
+                    full_ref.at[x, pl.ds(row4, 4), pl.ds(begin, HALF)],
+                    z_s.at[at],
+                    z_r.at[at],
+                    spot(x, y, (z + dz) % 8, (c + dc) % 2),
+                )
+                copy.start()
+                copies.append(copy)
     depart(1, 0)
     keep.wait()
-    swap.wait()
-    copies = []
-    for dz in (4, 3, 5, 2, 6, 1, 7):
-        block = full_ref.at[x, pl.ds(row, 8), pl.ds(mine, HALF)]
-        copy = remote(block, block, z_s.at[dz - 1], z_r.at[dz - 1], spot(x, y, (z + dz) % 8, c))
-        copy.start()
-        copies.append(copy)
     depart(1, 1)
     xhat, inv_scale = normalize(frames_ref[...].astype(f32))
     xhat_ref[...] = xhat
@@ -391,36 +390,48 @@
             scaled[n, ys] = (cots[n, ys].astype(f32) * weight).astype(bf)
             return carry
 
+        def hide(n, carry):
+            cols = columns_of(n, 256)
+            hidden = jnp.dot(slots[:, ys, :, 0:1024].reshape(256, 1024), inner[:, cols], preferred_element_type=f32)
+            sig = jax.nn.sigmoid(hidden)
+            active[:, ys, :, cols] = (hidden * sig).astype(bf).reshape(4, 64, 256)
+            slope_buf[:, cols] = sig * (1.0 + hidden * (1.0 - sig))
+            return carry
+
+        lax.fori_loop(0, 4, hide, 0)
+
+        def outward(n, carry):
+            cols = columns_of(n, 256)
+            out = jnp.dot(active[:, ys].reshape(256, 1024), outer[:, cols], preferred_element_type=f32)
+            part_y[q, :, :, cols] = out.astype(bf).reshape(4, 64, 256)
+            return carry
+
+        lax.fori_loop(0, 4, outward, 0)
+        push(2, q, part_y.at[q, far], relay_y.at[q], to_right)
+        push(1, q, part_y.at[q, left], straight_y.at[q], to_left)
         lax.fori_loop(0, 4, scale, 0)
 
-        def first(n, carry):
-            cols = pl.ds(pl.multiple_of(n * 256, 256), 256)
-            hidden = jnp.dot(slots[:, ys, :, 0:1024].reshape(256, 1024), inner[:, cols], preferred_element_type=f32)
+        def hide_back(n, carry):
+            cols = columns_of(n, 256)
             act_grad = lax.dot_general(
                 scaled[:, ys].reshape(256, 1024), outer[cols, :], (((1,), (1,)), ((), ())), preferred_element_type=f32
             )
-            sig = jax.nn.sigmoid(hidden)
-            active[:, ys, :, cols] = (hidden * sig).astype(bf).reshape(4, 64, 256)
-            slope = sig * (1.0 + hidden * (1.0 - sig))
-            pre[:, ys, :, cols] = (act_grad * slope).astype(bf).reshape(4, 64, 256)
+            pre[:, ys, :, cols] = (act_grad * slope_buf[:, cols]).astype(bf).reshape(4, 64, 256)
             return carry
 
-        lax.fori_loop(0, 4, first, 0)
-        def second(n, carry):
-            cols = pl.ds(pl.multiple_of(n * 256, 256), 256)
-            out = jnp.dot(active[:, ys].reshape(256, 1024), outer[:, cols], preferred_element_type=f32)
-            part_y[q, :, :, cols] = out.astype(bf).reshape(4, 64, 256)
+        lax.fori_loop(0, 4, hide_back, 0)
+
+        def outward_back(n, carry):
+            cols = columns_of(n, 256)
             out = lax.dot_general(
                 pre[:, ys].reshape(256, 1024), inner[cols, :], (((1,), (1,)), ((), ())), preferred_element_type=f32
             )
             part_z[q, :, :, cols] = out.astype(bf).reshape(4, 64, 256)
             return carry
 
-        lax.fori_loop(0, 4, second, 0)
-        push(2, q, part_y.at[q, far], relay_y.at[q], to_right)
+        lax.fori_loop(0, 4, outward_back, 0)
         push(3, q, part_z.at[q, far], relay_z.at[q], to_left)
         push(0, q, part_z.at[q, right], straight_z.at[q], to_right)
-        push(1, q, part_y.at[q, left], straight_y.at[q], to_left)
 
     def relay(q):
         folds[2, q].wait_recv()
@@ -432,31 +443,31 @@
 
     def deliver(q):
         yt = source_y(q)
-        for name in (1, 4, 0, 5):
-            folds[name, q].wait_recv()
-        part_y[q, x] = (part_y[q, x].astype(f32) + straight_y[q].astype(f32) + joint_y[q].astype(f32)).astype(bf)
-        part_z[q, x] = (part_z[q, x].astype(f32) + straight_z[q].astype(f32) + joint_z[q].astype(f32)).astype(bf)
-
-        def back(i, carry):
-            zt, ct = (z + 4 + i // 2) % 8, (c + i) % 2
-            rows = pl.ds(pl.multiple_of(8 * zt + 4 * ct, 4), 4)
-            for kind, (source, target) in enumerate(((part_y, y_ref), (part_z, z_ref))):
+        for kind, (source, target, straight, joint, names) in enumerate(
+            ((part_y, y_ref, straight_y, joint_y, (1, 4)), (part_z, z_ref, straight_z, joint_z, (0, 5)))
+        ):
+            for name in names:
+                folds[name, q].wait_recv()
+            source[q, x] = (source[q, x].astype(f32) + straight[q].astype(f32) + joint[q].astype(f32)).astype(bf)
+
+            def back(i, carry, kind=kind, source=source, target=target):
+                zt, ct = (z + 4 + i // 2) % 8, (c + i) % 2
+                rows = pl.ds(pl.multiple_of(8 * zt + 4 * ct, 4), 4)
                 remote(
                     source.at[q, x, rows], target.at[pl.ds(own4, 4)], back_s.at[kind], back_r.at[kind], (x, yt * 16 + zt * 2 + ct)
                 ).start()
-            return carry
-
-        if STEPS[q] == 0:
-            lax.fori_loop(0, 8, back, 0)
-            lax.fori_loop(9, 16, back, 0)
-            for kind, (source, target) in enumerate(((part_y, y_ref), (part_z, z_ref))):
+                return carry
+
+            if STEPS[q] == 0:
+                lax.fori_loop(0, 8, back, 0)
+                lax.fori_loop(9, 16, back, 0)
                 copy = pltpu.make_async_copy(
                     source.at[q, x, pl.ds(line4, 4)], target.at[pl.ds(own4, 4)], self_s.at[2 + kind]
                 )
                 copy.start()
                 selfs[2 + kind] = copy
-        else:
-            lax.fori_loop(0, 16, back, 0)
+            else:
+                lax.fori_loop(0, 16, back, 0)
 
     stores = []
 
@@ -544,11 +555,9 @@
 
     def depth_back(n, carry):
         cols = columns_of(n, 128)
-        grad = cg_buf[16:144, cols]
         total = jnp.zeros((128, 128), f32)
         for k in range(KERNEL):
             total = total + taps_ref[64 + k : 65 + k, cols] * cg_buf[31 - k : 159 - k, cols]
-            tg_buf[64 + k : 65 + k, cols] = jnp.sum(grad * gated_ref[k + 1 : k + 129, cols], axis=0, keepdims=True)
         total = total * mask
         sig = sig_ref[:, cols]
         pc_buf[:, cols] = (total * sig).astype(bf)
@@ -556,9 +565,13 @@
         return carry
 
     lax.fori_loop(0, 8, depth_back, 0)
-    out = lax.dot_general(mixed_ref[...], logit_grad, down, preferred_element_type=f32)
-    out = out + lax.dot_general(tg_buf[...].astype(bf), identity(), down, preferred_element_type=f32)
-    part_ref[:, :, 2048:2176] = out.astype(bf).reshape(4, 256, 128)
+
+    def depth_taps(n, carry):
+        cols = columns_of(n, 128)
+        grad = cg_buf[16:144, cols]
+        for k in range(KERNEL):
+            tg_buf[64 + k : 65 + k, cols] = jnp.sum(grad * gated_ref[k + 1 : k + 129, cols], axis=0, keepdims=True)
+        return carry
 
     def outer_product(i, carry):
         cols = columns_of((i + 9 * (1 - c)) % 16, 128)
@@ -576,8 +589,10 @@
         return slice(None), pl.ds(pl.multiple_of(index * 64, 64), 64)
 
     swaps = {}
-    for step in order:
-        for colour, (begin, width) in enumerate(colours):
+
+    def swap_out(colour):
+        begin, width = colours[colour]
+        for step in order:
             at = ((x if colour == 0 else y) + step) % 4
             lead, rows = rows_of(colour, at)
             slot = colour * 4 + step
@@ -591,6 +606,12 @@
             copy.start()
             swaps[colour, step] = copy
 
+    swap_out(0)
+    lax.fori_loop(0, 8, depth_taps, 0)
+    out = lax.dot_general(mixed_ref[...], logit_grad, down, preferred_element_type=f32)
+    out = out + lax.dot_general(tg_buf[...].astype(bf), identity(), down, preferred_element_type=f32)
+    part_ref[:, :, 2048:2176] = out.astype(bf).reshape(4, 256, 128)
+    swap_out(1)
     lax.fori_loop(9, 16, outer_product, 0)
 
     def inward(n, carry):
@@ -774,26 +795,29 @@
                 value = value + mid_near[colour, side, rows, pl.ds(0, width)].astype(jnp.float32)
             z_src[pl.ds(piece * 4, 4), :, pl.ds(begin, width)] = value.astype(jnp.bfloat16).reshape(4, 8, width)
     z_copies = []
-    for dz in (4, 3, 5, 2, 6, 1, 7):
-        to = (z + dz) % 8
-        copy = remote(z_src.at[to], z_buf.at[dz - 1], rz_s.at[dz - 1], rz_r.at[dz - 1], spot(x, y, to, c))
-        copy.start()
-        z_copies.append(copy)
-    total = z_src[z].astype(jnp.float32)
+    for dz in (4, 3, 5, 2, 6, 1, 7, 0):
+        for dc in (0, 1):
+            if dz or dc:
+                to, core = (z + dz) % 8, (c + dc) % 2
+                at = 2 * dz + dc
+                copy = remote(
+                    z_src.at[to, pl.ds(pl.multiple_of(4 * core, 4), 4)], z_buf.at[at], rz_s.at[at], rz_r.at[at], spot(x, y, to, core)
+                )
+                copy.start()
+                z_copies.append(copy)
+    own8 = z_src[z].astype(f32)
+    kept = jnp.where(c == 0, own8[0:4, :], own8[4:8, :])
     for copy in z_copies:
         copy.wait_recv()
-    for k in range(7):
-        total = total + z_buf[k].astype(jnp.float32)
-    last_src[...] = total
-    last = remote(last_src, last_buf, last_s, last_r, partner)
-    last.start()
+    got = jnp.zeros((4, HALF), f32)
+    for dz in range(8):
+        if dz:
+            kept = kept + z_buf[2 * dz].astype(f32)
+        got = got + z_buf[2 * dz + 1].astype(f32)
     for copy in sent + z_copies:
         copy.wait_send()
     for copy in swaps.values():
         copy.wait_send()
-    kept = jnp.where(c == 0, last_src[0:4, :], last_src[4:8, :])
-    last.wait()
-    got = jnp.where(c == 0, last_buf[0:4, :], last_buf[4:8, :])
     low, high = jnp.where(c == 0, kept, got), jnp.where(c == 0, got, kept)
     out_ref[:, 0:HALF] = low
     out_ref[:, HALF:2048] = high[:, 0 : 2048 - HALF]
@@ -840,12 +864,13 @@
         + [
             pltpu.VMEM((4, 256, WIDE), bf), pltpu.VMEM((4, 256, HALF), bf), half(2, 4, 256), half(2, 2, 128),
             half(2, 2, 256), half(2, 2, 64), half(2, 2, 32), half(2, 2, 64), pltpu.VMEM((8, 8, HALF), bf),
-            pltpu.VMEM((7, 8, HALF), bf), pltpu.VMEM((8, HALF), f32), pltpu.VMEM((8, HALF), f32),
+            pltpu.VMEM((16, 4, HALF), bf),
+            pltpu.VMEM((256, 1024), f32),
         ]
         + [
-            dma((2,)), dma, dma, dma, dma((7,)), dma((7,)), dma((16,)), dma((16,)), dma((8,)), dma((8,)),
+            dma((2,)), dma, dma((16,)), dma((16,)), dma((16,)), dma((16,)), dma((8,)), dma((8,)),
             dma((4,)), dma((2, 4)), dma((2, 4)), dma((2, 4, 4)), dma((2, 4, 4)), dma((6, 4)), dma((6, 4)), dma((2,)),
-            dma((2,)), dma((2,)), dma((8,)), dma((8,)), dma((24,)), dma((24,)), dma((7,)), dma((7,)), dma, dma,
+            dma((2,)), dma((2,)), dma((8,)), dma((8,)), dma((24,)), dma((24,)), dma((16,)), dma((16,)),
         ],
         compiler_params=pltpu.CompilerParams(
             collective_id=2, has_side_effects=True, vmem_limit_bytes=VMEM_LIMIT

time: 181 us -> 176 us (0.972)
  Pallas kernels: 180 us -> 175 us
    pallas_call x1, Pallas kernels: 175 us -> 171 us  [layer(): pl.pallas_call(layer_kernel, out_shape=(shape((128, 1024), bf), shape((12...]
where the time goes in v5:
time: 176 us
  Pallas kernels  175 us (99%)
    pallas_call x1, Pallas kernels, layer(): pl.pallas_call(layer_kernel, out_shape=(shape((128, 1024), bf), shape((12...  171 us
    pallas_call x1, Pallas kernels, pass_on(): pl.pallas_call(pass_kernel, out_shape=shapes, in_specs=[anywhere] * 7, ou...  4.13 us

profile of v5, /device:TPU:1, one launch (start us, length us, event | category | flops | bytes accessed | tf_op | source)
XLA Modules:
  0.0 176.4 jit_solution(16355858128301751249)
XLA Ops:
  1.3 170.9 %layer.1 = (bf16[128,1024]{1,0:T(8,128)(2,1)}, bf16[128,1024]{1,0:T(8,128)(2,1)}, f32[4,2048]{1,0:T(4,128)}, f32[4,31]{1,0:T(4,128)}, f32[4,64]{1,0:T(4,128)}, /...) custom-call(bf16[128,1024]{1,0:T(8,128)(2,1)} %frames_ref.1, s32[1]{0:T(128)S(6)} %copy.16.length_ref, ...), custom_call_target="tpu_custom_call" | custom-call | tf_op jit(solution)/shard_map/layer/pallas_call | solution.py:844
  172.2 4.1 %pass_on.1 = (bf16[128,1024]{1,0:T(8,128)(2,1)}, bf16[128,1024]{1,0:T(8,128)(2,1)}, f32[4,2048]{1,0:T(4,128)}, f32[4,31]{1,0:T(4,128)}, f32[4,64]{1,0:T(4,128)},...) custom-call(bf16[128,1024]{1,0:T(8,128)(2,1)} %get-tuple-element.21.refs_0_, ...), custom_call_target="tpu_custom_call" | custom-call | tf_op jit(solution)/shard_map/pass_on/pallas_call | solution.py:904

commit v6 on v5

--- a/solution.py
+++ b/solution.py
@@ -495,12 +495,12 @@
     forward(0, 0)
     arrive(0, 2)
     forward(0, 1)
-    compute(0)
     arrive(0, 3)
     forward(0, 2)
+    compute(0)
+    forward(0, 3)
     compute(1)
     relay(0)
-    forward(0, 3)
     compute(2)
     relay(1)
     deliver(0)

time: 176 us -> 175 us (level)
  no operation moved by 1% of the time
where the time goes in v6:
time: 175 us
  Pallas kernels  174 us (99%)
    pallas_call x1, Pallas kernels, layer(): pl.pallas_call(layer_kernel, out_shape=(shape((128, 1024), bf), shape((12...  170 us
    pallas_call x1, Pallas kernels, pass_on(): pl.pallas_call(pass_kernel, out_shape=shapes, in_specs=[anywhere] * 7, ou...  4.13 us

profile of v6, /device:TPU:1, one launch (start us, length us, event | category | flops | bytes accessed | tf_op | source)
XLA Modules:
  0.0 175.2 jit_solution(4085539274604516259)
XLA Ops:
  1.3 169.8 %layer.1 = (bf16[128,1024]{1,0:T(8,128)(2,1)}, bf16[128,1024]{1,0:T(8,128)(2,1)}, f32[4,2048]{1,0:T(4,128)}, f32[4,31]{1,0:T(4,128)}, f32[4,64]{1,0:T(4,128)}, /...) custom-call(bf16[128,1024]{1,0:T(8,128)(2,1)} %frames_ref.1, s32[1]{0:T(128)S(6)} %copy.16.length_ref, ...), custom_call_target="tpu_custom_call" | custom-call | tf_op jit(solution)/shard_map/layer/pallas_call | solution.py:844
  171.1 4.1 %pass_on.1 = (bf16[128,1024]{1,0:T(8,128)(2,1)}, bf16[128,1024]{1,0:T(8,128)(2,1)}, f32[4,2048]{1,0:T(4,128)}, f32[4,31]{1,0:T(4,128)}, f32[4,64]{1,0:T(4,128)},...) custom-call(bf16[128,1024]{1,0:T(8,128)(2,1)} %get-tuple-element.21.refs_0_, ...), custom_call_target="tpu_custom_call" | custom-call | tf_op jit(solution)/shard_map/pass_on/pallas_call | solution.py:904
